TPU v7x, 256 devices: a whole 4x4x8 slice. The times are simulated.
256 devices in a mesh: section: 32 (over y, z), dp: 8 (over x, core).
Axes of the slice: x: 4, y: 4, z: 8, core: 2. Of those that a mesh axis runs over, the one named last changes fastest.
Arguments:
- w_first: bfloat16 [32, 512, 2048], P('section'), may hold values from -0.25 to 0.25
- w_second_t: bfloat16 [32, 512, 2048], P('section'), may hold values from -0.125 to 0.125
- m_first: float32 [32, 512, 2048], P('section', 'dp'), may hold values from -6 to 6
- v_first: float32 [32, 512, 2048], P('section', 'dp'), may hold values from 10 to 100
- m_second: float32 [32, 512, 2048], P('section', 'dp'), may hold values from -6 to 6
- v_second: float32 [32, 512, 2048], P('section', 'dp'), may hold values from 10 to 100
- lengths: int32 [8, 34], replicated, may hold values from 1 to 256, 4352 in all within a row
- act_arrive: bfloat16 [8, 32, 256, 512], P('dp', 'section'), may hold values from -6 to 6
- cot_arrive: bfloat16 [8, 32, 256, 512], P('dp', 'section'), may hold values from -6 to 6
- embed_next: bfloat16 [8, 2, 256, 512], P('dp'), may hold values from -6 to 6
- loss_cot: bfloat16 [8, 2, 256, 512], P('dp'), may hold values from -6 to 6
- stash: bfloat16 [8, 32, 3, 256, 512], P('dp', 'section'), may hold values from -6 to 6
Outputs:
- act_leave: bfloat16 [8, 32, 3, 256, 512], P('dp', 'section')
- cot_leave: bfloat16 [8, 32, 3, 256, 512], P('dp', 'section')
- step_first: float32 [32, 512, 2048], P('section', 'dp')
- step_second: float32 [32, 512, 2048], P('section', 'dp')
Inputs may be any that keep to these rules, and one draw needn't show every extreme that they name: lengths[g, m] counts the live rows of microbatch m of data group g; each row of lengths sums to 4352 and its largest entry is 256.
All inputs are finite; a program needn't handle non-finite values.
Results may differ from a plain program's by a relative error of at most 0.007.
Values may be sent and summed in bfloat16 or wider, within the bound.
No kernel may reach another device: no remote copies, remote signals or barrier semaphores. Data moves between devices by JAX's collectives and lax.ppermute only.
A program may use at most 128 MiB of HBM per device.

v0:
```python
import jax
import jax.numpy as jnp
from jax import lax
from jax.experimental import pallas as pl
from jax.experimental.pallas import tpu as pltpu
from jax.sharding import PartitionSpec as P


D = 512
FF = 2048
ROWS = 256
CHUNK = 512
NORM_EPS = 1e-05
ADAM_EPS = 1e-08
BETA_ONE = 0.9
BETA_TWO = 0.98
CORRECT_ONE = 1.0 - 0.9**10
CORRECT_TWO = 1.0 - 0.98**10
GELU = 0.7978845608
CUBIC = 0.044715
ALPHA = 1500.0**0.25
F32 = jnp.float32
BF16 = jnp.bfloat16

VMEM = pl.BlockSpec(memory_space=pltpu.VMEM)
HBM = pl.BlockSpec(memory_space=pltpu.HBM)


def call(kernel, outs, *args, scratch=(), raw=(), out=VMEM, flops=0, limit=None):
    kernel_call = pl.pallas_call(
        kernel,
        out_shape=[jax.ShapeDtypeStruct(s, d) for s, d in outs],
        in_specs=[HBM if i in raw else VMEM for i in range(len(args))],
        out_specs=[out] * len(outs),
        scratch_shapes=list(scratch),
        cost_estimate=pl.CostEstimate(flops=flops, transcendentals=0, bytes_accessed=0),
        compiler_params=pltpu.CompilerParams(vmem_limit_bytes=limit or (16 << 20)),
    )
    args = [
        pltpu.with_memory_space_constraint(a, pltpu.HBM) if i in raw else a
        for i, a in enumerate(args)
    ]
    return kernel_call(*args)


def dot(a, b):
    return jnp.dot(a, b, preferred_element_type=F32)


def dot_t(a, b):
    return lax.dot_general(a, b, (((1,), (1,)), ((), ())), preferred_element_type=F32)


def chunks():
    return [slice(c, c + CHUNK) for c in range(0, FF, CHUNK)]


def gelu_both(pre):
    w = GELU + (GELU * CUBIC) * (pre * pre)
    a = 0.5 + 0.5 * jnp.tanh(pre * w)
    value = pre * a
    return value, a + value * (1.0 - a) * (6.0 * w - 4.0 * GELU)


def live(length):
    return lax.broadcasted_iota(jnp.int32, (ROWS, 128), 0) < length


def norm_parts(summed):
    center = summed - jnp.mean(summed, axis=1, keepdims=True)
    inv = lax.rsqrt(jnp.mean(center * center, axis=1, keepdims=True) + NORM_EPS)
    return center * inv, inv


def forward_tick(x, w1, w2, mask):
    acc = ALPHA * x.astype(F32)
    for c in chunks():
        h = gelu_both(dot(x, w1[0, :, c]))[0].astype(BF16)
        acc = acc + dot_t(h, w2[0, :, c])
    return jnp.where(mask()[:, :1] > 0.0, norm_parts(acc)[0], 0.0).astype(BF16)


def grad_of_sum(cot, normed, inv_live):
    g = cot.astype(F32)
    mean_g = jnp.mean(g, axis=1, keepdims=True)
    mean_gn = jnp.mean(g * normed, axis=1, keepdims=True)
    return inv_live * (g - mean_g - normed * mean_gn)


def back_zero_kernel(lens_hbm, w1_hbm, w2_hbm, stash_hbm, cot_hbm,
                     gin, gp, h, gs, w1, w2, x, slope, cot, lens, sem, w_sem):
    group, section = lax.axis_index("dp"), lax.axis_index("section")
    get_x = pltpu.make_async_copy(stash_hbm.at[0, 0, 0], x, sem.at[0])
    get_x.start()
    streams = [
        [
            pltpu.make_async_copy(src.at[0, :, c], dst.at[0, :, c], w_sem.at[j, i])
            for j, (src, dst) in enumerate(((w1_hbm, w1), (w2_hbm, w2)))
        ]
        for i, c in enumerate(chunks())
    ]
    get_lens = pltpu.make_async_copy(lens_hbm, lens, sem.at[1])
    get_cot = pltpu.make_async_copy(cot_hbm.at[0, 0], cot, sem.at[2])
    for pair in streams[:2]:
        for copy in pair:
            copy.start()
    get_lens.start()
    get_x.wait()
    acc = ALPHA * x[...].astype(F32)
    for i, c in enumerate(chunks()):
        get_w1, get_w2 = streams[i]
        get_w1.wait()
        if i + 2 < len(streams):
            streams[i + 2][0].start()
        if i == 1:
            get_cot.start()
        value, s = gelu_both(dot(x[...], w1[0, :, c]))
        value = value.astype(BF16)
        h[:, c] = value
        slope[:, c] = s
        get_w2.wait()
        if i + 2 < len(streams):
            streams[i + 2][1].start()
        acc = acc + dot_t(value, w2[0, :, c])
    normed, inv = norm_parts(acc)
    get_lens.wait()
    get_cot.wait()
    inv = jnp.where(live(lens[group, section])[:, :1], inv, 0.0)
    total = grad_of_sum(cot[...], normed, inv)
    total_b = total.astype(BF16)
    gs[...] = total_b
    acc = ALPHA * total
    for c in chunks():
        g = (dot(total_b, w2[0, :, c]) * slope[:, c]).astype(BF16)
        gp[:, c] = g
        acc = acc + dot_t(g, w1[0, :, c])
    gin[...] = acc.astype(BF16)


def prepare(k, w1, w2, stash, masks, h, slope, normed, inv):
    x = stash[0, 0, k]
    acc = ALPHA * x.astype(F32)
    for c in chunks():
        value, s = gelu_both(dot(x, w1[0, :, c]))
        value = value.astype(BF16)
        h[:, c] = value
        slope[:, c] = s
        acc = acc + dot_t(value, w2[0, :, c])
    nrm, inv_std = norm_parts(acc)
    normed[...] = nrm
    inv[...] = masks[k - 1] * inv_std


def prepare_one_kernel(*refs):
    prepare(1, *refs)


def prepare_two_kernel(*refs):
    prepare(2, *refs)


def back_one_kernel(w1, w2, passed, loss, slope, normed, inv, gin, gp, gs):
    cot = jnp.where(at_end(), loss[0, 0], passed[...])
    total = grad_of_sum(cot, normed[...], inv[:, :1])
    total_b = total.astype(BF16)
    gs[...] = total_b
    acc = ALPHA * total
    for c in chunks():
        g = (dot(total_b, w2[0, :, c]) * slope[:, c]).astype(BF16)
        gp[:, c] = g
        acc = acc + dot_t(g, w1[0, :, c])
    gin[...] = acc.astype(BF16)


def at_end():
    return lax.axis_index("section") == lax.axis_size("section") - 1


def owner_rows(ref):
    group = lax.axis_index("dp")
    chip, core = group // 2, group % 2
    parts = []
    for which in (core, 1 - core):
        for j in range(4):
            block = 2 * ((chip + j) % 4) + which
            parts.append(ref[pl.ds(pl.multiple_of(block * 64, 64), 64), :])
    return jnp.concatenate(parts, axis=0)


def terms_kernel(stash, gp0, gp1, gs0, gs1, h0, h1, first, second, x_rows, left):
    for i, a in enumerate((stash[0, 0, 0], stash[0, 0, 1], gs0[...], gs1[...], stash[0, 0, 2])):
        left[i] = jnp.transpose(a)
    a0, a1 = owner_rows(left.at[0]), owner_rows(left.at[1])
    for c in chunks():
        first[:, c] = dot(a0, gp0[:, c]) + dot(a1, gp1[:, c])
    a0, a1 = owner_rows(left.at[2]), owner_rows(left.at[3])
    for c in chunks():
        second[:, c] = dot(a0, h0[:, c]) + dot(a1, h1[:, c])
    x_rows[...] = owner_rows(left.at[4])


def back_two_kernel(passed, loss, normed, inv, h2, second, total_out, keep, send, left):
    cot = jnp.where(at_end(), loss[0, 1], passed[...])
    total = grad_of_sum(cot, normed[...], inv[:, :1])
    total_out[...] = total
    left[...] = jnp.transpose(total.astype(BF16))
    a = owner_rows(left)
    for c in chunks():
        r = second[:, c] + dot(a, h2[:, c])
        keep[:, c] = r[:256]
        send[:, c] = r[256:].astype(BF16)


def back_two_first_kernel(w2, total, slope, x_rows, first, gp, keep, send):
    total_b = total[...].astype(BF16)
    a = x_rows[...]
    for c in chunks():
        g = (dot(total_b, w2[0, :, c]) * slope[:, c]).astype(BF16)
        gp[:, c] = g
        r = first[:, c] + dot(a, g)
        keep[:, c] = r[:256]
        send[:, c] = r[256:].astype(BF16)


def leaving(leave, early, last, sem):
    copies = [
        pltpu.make_async_copy(src, leave.at[0, 0, k], sem.at[k])
        for k, src in enumerate(early + (last,))
    ]
    copies[0].start()
    copies[1].start()

    def finish():
        copies[2].start()
        for copy in copies:
            copy.wait()

    return finish


def back_leave_kernel(w1, total, gp, gin0, gin1, leave, gin2, sem):
    finish = leaving(leave, (gin0, gin1), gin2, sem)
    acc = ALPHA * total[...]
    for c in chunks():
        acc = acc + dot_t(gp[:, c], w1[0, :, c])
    gin2[...] = acc.astype(BF16)
    finish()


def forward_zero_kernel(lens_hbm, w1, w2, act, out, back_masks, masks, lens, sem):
    get_lens = pltpu.make_async_copy(lens_hbm, lens, sem)
    get_lens.start()
    group, section = lax.axis_index("dp"), lax.axis_index("section")
    last = lax.axis_size("section") - 1

    def mask():
        get_lens.wait()
        for k in (1, 2):
            back_masks[k - 1] = live(lens[group, section + k]).astype(F32)
            masks[k - 1] = live(lens[group, last - section + k]).astype(F32)
        return live(lens[group, last - section]).astype(F32)

    out[...] = forward_tick(act[0, 0], w1, w2, mask)


def forward_one_kernel(w1, w2, passed, embed, masks, out):
    x = jnp.where(lax.axis_index("section") == 0, embed[0, 0], passed[...])
    out[...] = forward_tick(x, w1, w2, lambda: masks[0])


def forward_two_kernel(w1, w2, passed, embed, masks, out0, out1, leave, out2, sem):
    finish = leaving(leave, (out0, out1), out2, sem)
    x = jnp.where(lax.axis_index("section") == 0, embed[0, 1], passed[...])
    out2[...] = forward_tick(x, w1, w2, lambda: masks[1])
    finish()


def ring_start_kernel(keep, got, up, down, mine, later):
    s = [keep[64 * j : 64 * j + 64] + got[64 * j : 64 * j + 64].astype(F32) for j in range(4)]
    up[:32] = s[2][:32].astype(BF16)
    up[32:] = s[1][32:].astype(BF16)
    down[:32] = s[2][32:].astype(BF16)
    down[32:] = s[3][:32].astype(BF16)
    mine[...] = s[0]
    later[:32] = s[1][:32]
    later[32:] = s[3][32:]


def ring_next_kernel(mine, later, got_up, got_down, up, down, part):
    up[...] = (later[:32] + got_up[:32].astype(F32)).astype(BF16)
    down[...] = (later[32:] + got_down[:32].astype(F32)).astype(BF16)
    part[:32] = mine[:32] + got_down[32:].astype(F32)
    part[32:] = mine[32:] + got_up[32:].astype(F32)


def adam_kernel(part, got_up, got_down, m, v, step, new, sem):
    copies = []
    for i in range(4):
        rows, got_rows = slice(16 * i, 16 * i + 16), slice(16 * (i % 2), 16 * (i % 2) + 16)
        g = part[rows] + (got_up, got_down)[i // 2][got_rows].astype(F32)
        m_new = BETA_ONE * m[0, rows] + (1.0 - BETA_ONE) * g
        v_new = BETA_TWO * v[0, rows] + (1.0 - BETA_TWO) * g * g
        new[rows] = m_new / CORRECT_ONE / (jnp.sqrt(v_new / CORRECT_TWO) + ADAM_EPS)
        copies.append(pltpu.make_async_copy(new.at[rows], step.at[0, rows], sem.at[i]))
        copies[i].start()
    for copy in copies:
        copy.wait()


def shifted(x, by):
    size = lax.axis_size("section")
    return lax.ppermute(x, "section", [(i, (i + by) % size) for i in range(size)])


def along_x(x, by):
    return lax.ppermute(x, "dp", [(i, ((i // 2 + by) % 4) * 2 + i % 2) for i in range(8)])


def other_core(x):
    return lax.ppermute(x, "dp", [(i, i ^ 1) for i in range(8)])


def window(
    w1, w2, m_first, v_first, m_second, v_second, lens, act, cot, embed, loss, stash
):
    mm = 2 * ROWS * D * FF
    small, wide, masks2 = (ROWS, D), (ROWS, FF), (2, ROWS, 128)
    lens_scratch = [pltpu.SMEM(lens.shape, jnp.int32)]

    gin0, gp0, h0, gs0, w1, w2 = call(
        back_zero_kernel,
        [(small, BF16), (wide, BF16), (wide, BF16), (small, BF16), (w1.shape, BF16), (w2.shape, BF16)],
        lens, w1, w2, stash, cot, raw=range(5), flops=4 * mm,
        scratch=[pltpu.VMEM(small, BF16), pltpu.VMEM(wide, F32), pltpu.VMEM(small, BF16)]
        + lens_scratch + [pltpu.SemaphoreType.DMA((3,)), pltpu.SemaphoreType.DMA((2, 4))],
    )
    back1 = shifted(gin0, -1)
    out0, back_masks, masks = call(
        forward_zero_kernel, [(small, BF16), (masks2, F32), (masks2, F32)], lens, w1, w2, act,
        raw=(0,), flops=2 * mm, scratch=lens_scratch + [pltpu.SemaphoreType.DMA],
    )
    ahead1 = shifted(out0, 1)

    def prepared(kernel):
        return call(
            kernel, [(wide, BF16), (wide, F32), (small, F32), ((ROWS, 128), F32)],
            w1, w2, stash, back_masks, flops=2 * mm,
        )

    h1, slope1, normed1, inv1 = prepared(prepare_one_kernel)
    gin1, gp1, gs1 = call(
        back_one_kernel, [(small, BF16), (wide, BF16), (small, BF16)],
        w1, w2, back1, loss, slope1, normed1, inv1, flops=2 * mm,
    )
    back2 = shifted(gin1, -1)
    h2, slope2, normed2, inv2 = prepared(prepare_two_kernel)
    acc_first, acc_second, x_rows = call(
        terms_kernel, [((D, FF), F32), ((D, FF), F32), ((D, ROWS), BF16)],
        stash, gp0, gp1, gs0, gs1, h0, h1, flops=4 * mm,
        scratch=[pltpu.VMEM((5, D, ROWS), BF16)],
    )
    total2, keep_second, send_second = call(
        back_two_kernel, [(small, F32), ((256, FF), F32), ((256, FF), BF16)],
        back2, loss, normed2, inv2, h2, acc_second, flops=mm,
        scratch=[pltpu.VMEM((D, ROWS), BF16)],
    )
    got_second = other_core(send_second)
    gp2, keep_first, send_first = call(
        back_two_first_kernel, [(wide, BF16), ((256, FF), F32), ((256, FF), BF16)],
        w2, total2, slope2, x_rows, acc_first, flops=2 * mm,
    )
    got_first = other_core(send_first)
    (out1,) = call(
        forward_one_kernel, [(small, BF16)], w1, w2, ahead1, embed, masks, flops=2 * mm
    )
    ahead2 = shifted(out1, 1)

    def ring_start(keep, got):
        return call(
            ring_start_kernel,
            [((64, FF), BF16), ((64, FF), BF16), ((64, FF), F32), ((64, FF), F32)], keep, got,
        )

    def ring_next(mine, later, got_up, got_down):
        return call(
            ring_next_kernel, [((32, FF), BF16), ((32, FF), BF16), ((64, FF), F32)],
            mine, later, got_up, got_down,
        )

    def adam(part, got_up, got_down, m, v):
        return call(
            adam_kernel, [((1, 64, FF), F32)], part, got_up, got_down, m, v, out=HBM,
            scratch=[pltpu.VMEM((64, FF), F32), pltpu.SemaphoreType.DMA((4,))],
        )[0]

    def both_ways(up, down):
        up = along_x(up, 1)
        down = along_x(down, -1)
        return up, down

    out_scratch = [pltpu.VMEM(small, BF16), pltpu.SemaphoreType.DMA((3,))]
    up_s, down_s, mine_s, later_s = ring_start(keep_second, got_second)
    up_s, down_s = both_ways(up_s, down_s)
    up_f, down_f, mine_f, later_f = ring_start(keep_first, got_first)
    up_f, down_f = both_ways(up_f, down_f)
    up_s, down_s, part_s = ring_next(mine_s, later_s, up_s, down_s)
    up_s, down_s = both_ways(up_s, down_s)
    (cot_leave,) = call(
        back_leave_kernel, [((1, 1, 3) + small, BF16)], w1, total2, gp2, gin0, gin1,
        out=HBM, flops=mm, scratch=out_scratch,
    )
    up_f, down_f, part_f = ring_next(mine_f, later_f, up_f, down_f)
    up_f, down_f = both_ways(up_f, down_f)
    (act_leave,) = call(
        forward_two_kernel, [((1, 1, 3) + small, BF16)], w1, w2, ahead2, embed, masks, out0, out1,
        out=HBM, flops=2 * mm, scratch=out_scratch,
    )
    step_second = adam(part_s, up_s, down_s, m_second, v_second)
    step_first = adam(part_f, up_f, down_f, m_first, v_first)
    return (act_leave, cot_leave, step_first, step_second)


def solution(mesh):
    by_section = P("section", None, None)
    by_rows = P("section", "dp", None)
    by_group = P("dp", "section", None, None)
    ticks = P("dp", "section", None, None, None)
    every = P("dp", None, None, None)
    return jax.shard_map(
        window,
        mesh=mesh,
        in_specs=(by_section, by_section, by_rows, by_rows, by_rows, by_rows, P(),
                  by_group, by_group, every, every, ticks),
        out_specs=(ticks, ticks, by_rows, by_rows),
        check_vma=False,
    )
```

profile of v0, /device:TPU:6, one launch (start us, length us, event | category | flops | bytes accessed | tf_op | source)
XLA Modules:
  0.0 67.8 jit_solution(11387148914405012697)
XLA Ops:
  0.6 6.3 %shard_map.147 = (bf16[256,512]{1,0:T(8,128)(2,1)S(1)}, bf16[256,2048]{1,0:T(8,128)(2,1)S(1)}, bf16[256,2048]{1,0:T(8,128)(2,1)S(1)}, bf16[256,512]{1,0:T(8,128)...) custom-call(s32[8,34]{1,0:T(8,128)} %lens_hbm.3, bf16[1,512,2048]{2,1,0:T(8,128)(2,1)} %w1_hbm.1, ...), custom_call_target="tpu_custom_call" | custom-call | flops 2147483648 | tf_op jit(solution)/shard_map/pallas_call | solution.py:43
  7.0 8.4 %collective-permute-start.2 = (bf16[256,512]{1,0:T(8,128)(2,1)S(1)}, bf16[256,512]{1,0:T(8,128)(2,1)S(1)}, u32[]{:S(2)}, u32[]{:S(2)}) collective-permute-start(bf16[256,512]{1,0:T(8,128)(2,1)S(1)} %get-tuple-element.51.gin0), channel_id=1, source_target_pairs={{0,248},{8,0},{16,8},{24,16},{32,24},{40,32},{48,40},{56,48},{64,5... | collective-permute-start | bytes 786440 | tf_op jit(solution)/shard_map/ppermute | solution.py:312
  15.3 2.1 %shard_map.148 = (bf16[256,512]{1,0:T(8,128)(2,1)S(1)}, f32[2,256,128]{2,1,0:T(8,128)S(1)}, f32[2,256,128]{2,1,0:T(8,128)S(1)}) custom-call(s32[8,34]{1,0:T(8,128)} %lens_hbm.3, bf16[1,512,2048]{2,1,0:T(8,128)(2,1)S(1)} %get-tuple-element.47.w1.refs_0_, bf16[1,512,2048]{2,1,0:T(8,128)(2,1)S(1)} %get-tuple-element.48.w2.refs_1_, ...), custom_call_target="tpu_custom_call" | custom-call | flops 1073741824 | tf_op jit(solution)/shard_map/pallas_call | solution.py:43
  17.5 2.4 %shard_map.151 = (bf16[256,2048]{1,0:T(8,128)(2,1)S(1)}, f32[256,2048]{1,0:T(8,128)S(1)}, f32[256,512]{1,0:T(8,128)S(1)}, f32[256,128]{1,0:T(8,128)S(1)}) custom-call(bf16[1,512,2048]{2,1,0:T(8,128)(2,1)S(1)} %get-tuple-element.47.w1.refs_0_, bf16[1,512,2048]{2,1,0:T(8,128)(2,1)S(1)} %get-tuple-element.48.w2.refs_1_, ...), custom_call_target="tpu_custom_call" | custom-call | flops 1073741824 | tf_op jit(solution)/shard_map/pallas_call | solution.py:43
  19.9 1.0 %collective-permute-done.2.passed = bf16[256,512]{1,0:T(8,128)(2,1)S(1)} collective-permute-done((bf16[256,512]{1,0:T(8,128)(2,1)S(1)}, bf16[256,512]{1,0:T(8,128)(2,1)S(1)}, u32[]{:S(2)}, u32[]{:S(2)}) %collective-permute-start.2) | collective-permute-done | bytes 262176 | tf_op jit(solution)/shard_map/ppermute | solution.py:312
  20.9 1.7 %shard_map.152 = (bf16[256,512]{1,0:T(8,128)(2,1)S(1)}, bf16[256,2048]{1,0:T(8,128)(2,1)S(1)}, bf16[256,512]{1,0:T(8,128)(2,1)S(1)}) custom-call(bf16[1,512,2048]{2,1,0:T(8,128)(2,1)S(1)} %get-tuple-element.47.w1.refs_0_, bf16[1,512,2048]{2,1,0:T(8,128)(2,1)S(1)} %get-tuple-element.48.w2.refs_1_, bf16[256,512]{1,0:T(8,128)(2,1)S(1)} %collective-permute-done.2.passed, ...), custom_call_target="tpu_custom_call" | custom-call | flops 1073741824 | tf_op jit(solution)/shard_map/pallas_call | solution.py:43
  22.7 6.1 %collective-permute-start.3 = (bf16[256,512]{1,0:T(8,128)(2,1)S(1)}, bf16[256,512]{1,0:T(8,128)(2,1)S(1)}, u32[]{:S(2)}, u32[]{:S(2)}) collective-permute-start(bf16[256,512]{1,0:T(8,128)(2,1)S(1)} %get-tuple-element.56.gin1), channel_id=1, source_target_pairs={{0,248},{8,0},{16,8},{24,16},{32,24},{40,32},{48,40},{56,48},{64,5... | collective-permute-start | bytes 786440 | tf_op jit(solution)/shard_map/ppermute | solution.py:312
  28.7 2.4 %shard_map.153 = (bf16[256,2048]{1,0:T(8,128)(2,1)S(1)}, f32[256,2048]{1,0:T(8,128)S(1)}, f32[256,512]{1,0:T(8,128)S(1)}, f32[256,128]{1,0:T(8,128)S(1)}) custom-call(bf16[1,512,2048]{2,1,0:T(8,128)(2,1)S(1)} %get-tuple-element.47.w1.refs_0_, bf16[1,512,2048]{2,1,0:T(8,128)(2,1)S(1)} %get-tuple-element.48.w2.refs_1_, ...), custom_call_target="tpu_custom_call" | custom-call | flops 1073741824 | tf_op jit(solution)/shard_map/pallas_call | solution.py:43
  31.2 2.7 %shard_map.154 = (f32[512,2048]{1,0:T(8,128)S(1)}, f32[512,2048]{1,0:T(8,128)S(1)}, bf16[512,256]{1,0:T(8,128)(2,1)S(1)}) custom-call(bf16[1,1,3,256,512]{4,3,2,1,0:T(8,128)(2,1)S(1)} %copy-done, bf16[256,2048]{1,0:T(8,128)(2,1)S(1)} %get-tuple-element.60.gp0, bf16[256,2048]{1,0:T(8,128)(2,1)S(1)} %get-tuple-element.61.gp1, ...), custom_call_target="tpu_custom_call" | custom-call | flops 2147483648 | tf_op jit(solution)/shard_map/pallas_call | solution.py:43
  33.9 1.0 %shard_map.155 = (f32[256,512]{1,0:T(8,128)S(1)}, f32[256,2048]{1,0:T(8,128)S(1)}, bf16[256,2048]{1,0:T(8,128)(2,1)S(1)}) custom-call(bf16[256,512]{1,0:T(8,128)(2,1)S(1)} %collective-permute-done.3.passed, bf16[1,2,256,512]{3,2,1,0:T(8,128)(2,1)S(1)} %copy-done.2, f32[256,512]{1,0:T(8,128)S(1)} %get-tuple-element.57.normed, ...), custom_call_target="tpu_custom_call" | custom-call | flops 536870912 | tf_op jit(solution)/shard_map/pallas_call | solution.py:43
  34.9 0.1 collective-permute-start.9
  35.0 1.8 %shard_map.156 = (bf16[256,2048]{1,0:T(8,128)(2,1)S(1)}, f32[256,2048]{1,0:T(8,128)S(1)}, bf16[256,2048]{1,0:T(8,128)(2,1)S(1)}) custom-call(bf16[1,512,2048]{2,1,0:T(8,128)(2,1)S(1)} %get-tuple-element.48.w2.refs_1_, f32[256,512]{1,0:T(8,128)S(1)} %get-tuple-element.67.total, f32[256,2048]{1,0:T(8,128)S(1)} %get-tuple-element.68.slope, ...), custom_call_target="tpu_custom_call" | custom-call | flops 1073741824 | tf_op jit(solution)/shard_map/pallas_call | solution.py:43
  36.8 0.6 collective-permute-start.4
  37.4 0.3 collective-permute-done.9.got
  37.7 0.2 shard_map.161
  37.9 0.6 collective-permute-start.10
  38.4 1.5 %collective-permute-start.11 = (bf16[64,2048]{1,0:T(8,128)(2,1)S(1)}, bf16[64,2048]{1,0:T(8,128)(2,1)S(1)}, u32[]{:S(2)}, u32[]{:S(2)}) collective-permute-start(bf16[64,2048]{1,0:T(8,128)(2,1)S(1)} %get-tuple-element.86), channel_id=1, source_target_pairs={{0,6},{1,7},{2,0},{3,1},{4,2},{5,3},{6,4},{7,5},{8,14},{9,15},{10,... | collective-permute-start | bytes 786440 | tf_op jit(solution)/shard_map/ppermute | solution.py:316
  40.0 0.2 shard_map.158
  40.1 1.8 %collective-permute-start.5 = (bf16[64,2048]{1,0:T(8,128)(2,1)S(1)}, bf16[64,2048]{1,0:T(8,128)(2,1)S(1)}, u32[]{:S(2)}, u32[]{:S(2)}) collective-permute-start(bf16[64,2048]{1,0:T(8,128)(2,1)S(1)} %get-tuple-element.76), channel_id=1, source_target_pairs={{0,2},{1,3},{2,4},{3,5},{4,6},{5,7},{6,0},{7,1},{8,10},{9,11},{10,... | collective-permute-start | bytes 786440 | tf_op jit(solution)/shard_map/ppermute | solution.py:316
  41.9 0.3 collective-permute-start.6
  42.2 7.1 %collective-permute-done.passed = bf16[256,512]{1,0:T(8,128)(2,1)S(1)} collective-permute-done((bf16[256,512]{1,0:T(8,128)(2,1)S(1)}, bf16[256,512]{1,0:T(8,128)(2,1)S(1)}, u32[]{:S(2)}, u32[]{:S(2)}) %collective-permute-start) | collective-permute-done | bytes 262176 | tf_op jit(solution)/shard_map/ppermute | solution.py:312
  49.3 2.0 %shard_map.149.out1 = bf16[256,512]{1,0:T(8,128)(2,1)S(1)} custom-call(bf16[1,512,2048]{2,1,0:T(8,128)(2,1)S(1)} %get-tuple-element.47.w1.refs_0_, bf16[1,512,2048]{2,1,0:T(8,128)(2,1)S(1)} %get-tuple-element.48.w2.refs_1_, bf16[256,512]{1,0:T(8,128)(2,1)S(1)} %collective-permute-done.passed, bf16[1,2,256,512]{3,2,1,0:T(8,128)(2,1)S(1)} %copy-done.1, ...), custom_call_target="tpu_custom_call" | custom-call | flops 1073741824 | tf_op jit(solution)/shard_map/pallas_call | solution.py:43
  51.5 0.6 collective-permute-start.12
  52.1 1.5 %collective-permute-start.13 = (bf16[32,2048]{1,0:T(8,128)(2,1)S(1)}, bf16[32,2048]{1,0:T(8,128)(2,1)S(1)}, u32[]{:S(2)}, u32[]{:S(2)}) collective-permute-start(bf16[32,2048]{1,0:T(8,128)(2,1)S(1)} %get-tuple-element.89), channel_id=1, source_target_pairs={{0,6},{1,7},{2,0},{3,1},{4,2},{5,3},{6,4},{7,5},{8,14},{9,15},{10,... | collective-permute-start | bytes 393224 | tf_op jit(solution)/shard_map/ppermute | solution.py:316
  53.7 1.8 %collective-permute-start.7 = (bf16[32,2048]{1,0:T(8,128)(2,1)S(1)}, bf16[32,2048]{1,0:T(8,128)(2,1)S(1)}, u32[]{:S(2)}, u32[]{:S(2)}) collective-permute-start(bf16[32,2048]{1,0:T(8,128)(2,1)S(1)} %get-tuple-element.79), channel_id=1, source_target_pairs={{0,2},{1,3},{2,4},{3,5},{4,6},{5,7},{6,0},{7,1},{8,10},{9,11},{10,... | collective-permute-start | bytes 393224 | tf_op jit(solution)/shard_map/ppermute | solution.py:316
  55.5 0.3 collective-permute-start.8
  55.8 1.5 %shard_map.157 = bf16[1,1,3,256,512]{4,3,2,1,0:T(8,128)(2,1)} custom-call(bf16[1,512,2048]{2,1,0:T(8,128)(2,1)S(1)} %get-tuple-element.47.w1.refs_0_, f32[256,512]{1,0:T(8,128)S(1)} %get-tuple-element.67.total, bf16[256,2048]{1,0:T(8,128)(2,1)S(1)} %get-tuple-element.71.gp, bf16[256,512]{1,0:T(8,128)(2,1)S(1)} %get-tuple-element.51.gin0, ...), custom_call_target="tpu_custom_call" | custom-call | flops 536870912 | tf_op jit(solution)/shard_map/pallas_call | solution.py:43
  57.3 5.1 %collective-permute-done.1.passed = bf16[256,512]{1,0:T(8,128)(2,1)S(1)} collective-permute-done((bf16[256,512]{1,0:T(8,128)(2,1)S(1)}, bf16[256,512]{1,0:T(8,128)(2,1)S(1)}, u32[]{:S(2)}, u32[]{:S(2)}) %collective-permute-start.1) | collective-permute-done | bytes 262176 | tf_op jit(solution)/shard_map/ppermute | solution.py:312
  62.4 2.7 %shard_map.150 = bf16[1,1,3,256,512]{4,3,2,1,0:T(8,128)(2,1)} custom-call(bf16[1,512,2048]{2,1,0:T(8,128)(2,1)S(1)} %get-tuple-element.47.w1.refs_0_, bf16[1,512,2048]{2,1,0:T(8,128)(2,1)S(1)} %get-tuple-element.48.w2.refs_1_, bf16[256,512]{1,0:T(8,128)(2,1)S(1)} %collective-permute-done.1.passed, bf16[1,2,256,512]{3,2,1,0:T(8,128)(2,1)S(1)} %copy-done.1, ...), custom_call_target="tpu_custom_call" | custom-call | flops 1073741824 | tf_op jit(solution)/shard_map/pallas_call | solution.py:43
  65.2 1.1 %shard_map.163 = f32[1,64,2048]{2,1,0:T(8,128)} custom-call(f32[64,2048]{1,0:T(8,128)S(1)} %get-tuple-element.87.part, bf16[32,2048]{1,0:T(8,128)(2,1)S(1)} %collective-permute-done.12.got_up, bf16[32,2048]{1,0:T(8,128)(2,1)S(1)} %collective-permute-done.13.got_down, f32[1,64,2048]{2,1,0:T(8,128)S(1)} %copy-done.3, f32[1,64,2048]{2,1,0:T(8,128)S(1)} %copy-done.4), custom_call_target="tpu_custom_call" | custom-call | tf_op jit(solution)/shard_map/pallas_call | solution.py:43
  66.3 0.2 copy-done.6
  66.5 1.1 %shard_map.160 = f32[1,64,2048]{2,1,0:T(8,128)} custom-call(f32[64,2048]{1,0:T(8,128)S(1)} %get-tuple-element.78.part, bf16[32,2048]{1,0:T(8,128)(2,1)S(1)} %collective-permute-done.7.got_up, bf16[32,2048]{1,0:T(8,128)(2,1)S(1)} %collective-permute-done.8.got_down, f32[1,64,2048]{2,1,0:T(8,128)S(1)} %copy-done.5, f32[1,64,2048]{2,1,0:T(8,128)S(1)} %copy-done.6), custom_call_target="tpu_custom_call" | custom-call | tf_op jit(solution)/shard_map/pallas_call | solution.py:43
  (29 shorter events, 0.3 us)
Async XLA Ops:
  0.6 14.7 %copy-start.7 = (bf16[1,1,256,512]{3,2,1,0:T(8,128)(2,1)S(1)}, bf16[1,1,256,512]{3,2,1,0:T(8,128)(2,1)}, u32[]{:S(2)}) copy-start(bf16[1,1,256,512]{3,2,1,0:T(8,128)(2,1)} %act.1) | copy-start | bytes 786436
  7.0 13.9 %collective-permute-start.2 = (bf16[256,512]{1,0:T(8,128)(2,1)S(1)}, bf16[256,512]{1,0:T(8,128)(2,1)S(1)}, u32[]{:S(2)}, u32[]{:S(2)}) collective-permute-start(bf16[256,512]{1,0:T(8,128)(2,1)S(1)} %get-tuple-element.51.gin0), channel_id=1, source_target_pairs={{0,248},{8,0},{16,8},{24,16},{32,24},{40,32},{48,40},{56,48},{64,5... | collective-permute-start | bytes 786440 | tf_op jit(solution)/shard_map/ppermute | solution.py:312
  15.3 2.1 %copy-start = (bf16[1,1,3,256,512]{4,3,2,1,0:T(8,128)(2,1)S(1)}, bf16[1,1,3,256,512]{4,3,2,1,0:T(8,128)(2,1)}, u32[]{:S(2)}) copy-start(bf16[1,1,3,256,512]{4,3,2,1,0:T(8,128)(2,1)} %stash.1) | copy-start | bytes 2359300
  17.5 3.5 %copy-start.2 = (bf16[1,2,256,512]{3,2,1,0:T(8,128)(2,1)S(1)}, bf16[1,2,256,512]{3,2,1,0:T(8,128)(2,1)}, u32[]{:S(2)}) copy-start(bf16[1,2,256,512]{3,2,1,0:T(8,128)(2,1)} %loss.3) | copy-start | bytes 1572868
  22.7 11.2 %collective-permute-start.3 = (bf16[256,512]{1,0:T(8,128)(2,1)S(1)}, bf16[256,512]{1,0:T(8,128)(2,1)S(1)}, u32[]{:S(2)}, u32[]{:S(2)}) collective-permute-start(bf16[256,512]{1,0:T(8,128)(2,1)S(1)} %get-tuple-element.56.gin1), channel_id=1, source_target_pairs={{0,248},{8,0},{16,8},{24,16},{32,24},{40,32},{48,40},{56,48},{64,5... | collective-permute-start | bytes 786440 | tf_op jit(solution)/shard_map/ppermute | solution.py:312
  34.9 2.7 %collective-permute-start.9 = (bf16[256,2048]{1,0:T(8,128)(2,1)S(1)}, bf16[256,2048]{1,0:T(8,128)(2,1)S(1)}, u32[]{:S(2)}, u32[]{:S(2)}) collective-permute-start(bf16[256,2048]{1,0:T(8,128)(2,1)S(1)} %get-tuple-element.82), channel_id=1, source_target_pairs={{0,1},{1,0},{2,3},{3,2},{4,5},{5,4},{6,7},{7,6},{8,9},{9,8},{10,11... | collective-permute-start | bytes 3145736 | tf_op jit(solution)/shard_map/ppermute | solution.py:320
  36.8 3.1 %collective-permute-start.4 = (bf16[256,2048]{1,0:T(8,128)(2,1)S(1)}, bf16[256,2048]{1,0:T(8,128)(2,1)S(1)}, u32[]{:S(2)}, u32[]{:S(2)}) collective-permute-start(bf16[256,2048]{1,0:T(8,128)(2,1)S(1)} %get-tuple-element.73), channel_id=1, source_target_pairs={{0,1},{1,0},{2,3},{3,2},{4,5},{5,4},{6,7},{7,6},{8,9},{9,8},{10,11... | collective-permute-start | bytes 3145736 | tf_op jit(solution)/shard_map/ppermute | solution.py:320
  37.4 11.9 %collective-permute-start = (bf16[256,512]{1,0:T(8,128)(2,1)S(1)}, bf16[256,512]{1,0:T(8,128)(2,1)S(1)}, u32[]{:S(2)}, u32[]{:S(2)}) collective-permute-start(bf16[256,512]{1,0:T(8,128)(2,1)S(1)} %get-tuple-element.49.out0), channel_id=1, source_target_pairs={{0,8},{8,16},{16,24},{24,32},{32,40},{40,48},{48,56},{56,64},{64,7... | collective-permute-start | bytes 786440 | tf_op jit(solution)/shard_map/ppermute | solution.py:312
  37.8 11.5 %copy-start.1 = (bf16[1,2,256,512]{3,2,1,0:T(8,128)(2,1)S(1)}, bf16[1,2,256,512]{3,2,1,0:T(8,128)(2,1)}, u32[]{:S(2)}) copy-start(bf16[1,2,256,512]{3,2,1,0:T(8,128)(2,1)} %embed.3) | copy-start | bytes 1572868
  37.9 13.5 %collective-permute-start.10 = (bf16[64,2048]{1,0:T(8,128)(2,1)S(1)}, bf16[64,2048]{1,0:T(8,128)(2,1)S(1)}, u32[]{:S(2)}, u32[]{:S(2)}) collective-permute-start(bf16[64,2048]{1,0:T(8,128)(2,1)S(1)} %get-tuple-element.85), channel_id=1, source_target_pairs={{0,2},{1,3},{2,4},{3,5},{4,6},{5,7},{6,0},{7,1},{8,10},{9,11},{10,... | collective-permute-start | bytes 786440 | tf_op jit(solution)/shard_map/ppermute | solution.py:316
  38.4 13.0 %collective-permute-start.11 = (bf16[64,2048]{1,0:T(8,128)(2,1)S(1)}, bf16[64,2048]{1,0:T(8,128)(2,1)S(1)}, u32[]{:S(2)}, u32[]{:S(2)}) collective-permute-start(bf16[64,2048]{1,0:T(8,128)(2,1)S(1)} %get-tuple-element.86), channel_id=1, source_target_pairs={{0,6},{1,7},{2,0},{3,1},{4,2},{5,3},{6,4},{7,5},{8,14},{9,15},{10,... | collective-permute-start | bytes 786440 | tf_op jit(solution)/shard_map/ppermute | solution.py:316
  40.1 13.5 %collective-permute-start.5 = (bf16[64,2048]{1,0:T(8,128)(2,1)S(1)}, bf16[64,2048]{1,0:T(8,128)(2,1)S(1)}, u32[]{:S(2)}, u32[]{:S(2)}) collective-permute-start(bf16[64,2048]{1,0:T(8,128)(2,1)S(1)} %get-tuple-element.76), channel_id=1, source_target_pairs={{0,2},{1,3},{2,4},{3,5},{4,6},{5,7},{6,0},{7,1},{8,10},{9,11},{10,... | collective-permute-start | bytes 786440 | tf_op jit(solution)/shard_map/ppermute | solution.py:316
  41.9 11.7 %collective-permute-start.6 = (bf16[64,2048]{1,0:T(8,128)(2,1)S(1)}, bf16[64,2048]{1,0:T(8,128)(2,1)S(1)}, u32[]{:S(2)}, u32[]{:S(2)}) collective-permute-start(bf16[64,2048]{1,0:T(8,128)(2,1)S(1)} %get-tuple-element.77), channel_id=1, source_target_pairs={{0,6},{1,7},{2,0},{3,1},{4,2},{5,3},{6,4},{7,5},{8,14},{9,15},{10,... | collective-permute-start | bytes 786440 | tf_op jit(solution)/shard_map/ppermute | solution.py:316
  51.3 11.1 %collective-permute-start.1 = (bf16[256,512]{1,0:T(8,128)(2,1)S(1)}, bf16[256,512]{1,0:T(8,128)(2,1)S(1)}, u32[]{:S(2)}, u32[]{:S(2)}) collective-permute-start(bf16[256,512]{1,0:T(8,128)(2,1)S(1)} %shard_map.149.out1), channel_id=1, source_target_pairs={{0,8},{8,16},{16,24},{24,32},{32,40},{40,48},{48,56},{56,64},{64,7... | collective-permute-start | bytes 786440 | tf_op jit(solution)/shard_map/ppermute | solution.py:312
  51.5 13.7 %collective-permute-start.12 = (bf16[32,2048]{1,0:T(8,128)(2,1)S(1)}, bf16[32,2048]{1,0:T(8,128)(2,1)S(1)}, u32[]{:S(2)}, u32[]{:S(2)}) collective-permute-start(bf16[32,2048]{1,0:T(8,128)(2,1)S(1)} %get-tuple-element.88), channel_id=1, source_target_pairs={{0,2},{1,3},{2,4},{3,5},{4,6},{5,7},{6,0},{7,1},{8,10},{9,11},{10,... | collective-permute-start | bytes 393224 | tf_op jit(solution)/shard_map/ppermute | solution.py:316
  52.1 13.1 %collective-permute-start.13 = (bf16[32,2048]{1,0:T(8,128)(2,1)S(1)}, bf16[32,2048]{1,0:T(8,128)(2,1)S(1)}, u32[]{:S(2)}, u32[]{:S(2)}) collective-permute-start(bf16[32,2048]{1,0:T(8,128)(2,1)S(1)} %get-tuple-element.89), channel_id=1, source_target_pairs={{0,6},{1,7},{2,0},{3,1},{4,2},{5,3},{6,4},{7,5},{8,14},{9,15},{10,... | collective-permute-start | bytes 393224 | tf_op jit(solution)/shard_map/ppermute | solution.py:316
  53.7 12.6 %collective-permute-start.7 = (bf16[32,2048]{1,0:T(8,128)(2,1)S(1)}, bf16[32,2048]{1,0:T(8,128)(2,1)S(1)}, u32[]{:S(2)}, u32[]{:S(2)}) collective-permute-start(bf16[32,2048]{1,0:T(8,128)(2,1)S(1)} %get-tuple-element.79), channel_id=1, source_target_pairs={{0,2},{1,3},{2,4},{3,5},{4,6},{5,7},{6,0},{7,1},{8,10},{9,11},{10,... | collective-permute-start | bytes 393224 | tf_op jit(solution)/shard_map/ppermute | solution.py:316
  55.5 10.8 %collective-permute-start.8 = (bf16[32,2048]{1,0:T(8,128)(2,1)S(1)}, bf16[32,2048]{1,0:T(8,128)(2,1)S(1)}, u32[]{:S(2)}, u32[]{:S(2)}) collective-permute-start(bf16[32,2048]{1,0:T(8,128)(2,1)S(1)} %get-tuple-element.80), channel_id=1, source_target_pairs={{0,6},{1,7},{2,0},{3,1},{4,2},{5,3},{6,4},{7,5},{8,14},{9,15},{10,... | collective-permute-start | bytes 393224 | tf_op jit(solution)/shard_map/ppermute | solution.py:316
  57.3 7.9 %copy-start.3 = (f32[1,64,2048]{2,1,0:T(8,128)S(1)}, f32[1,64,2048]{2,1,0:T(8,128)}, u32[]{:S(2)}) copy-start(f32[1,64,2048]{2,1,0:T(8,128)} %m.3) | copy-start | bytes 1572868
  57.3 7.9 %copy-start.4 = (f32[1,64,2048]{2,1,0:T(8,128)S(1)}, f32[1,64,2048]{2,1,0:T(8,128)}, u32[]{:S(2)}) copy-start(f32[1,64,2048]{2,1,0:T(8,128)} %v.3) | copy-start | bytes 1572868
  65.2 1.2 %copy-start.5 = (f32[1,64,2048]{2,1,0:T(8,128)S(1)}, f32[1,64,2048]{2,1,0:T(8,128)}, u32[]{:S(2)}) copy-start(f32[1,64,2048]{2,1,0:T(8,128)} %m.2) | copy-start | bytes 1572868
  65.2 1.4 %copy-start.6 = (f32[1,64,2048]{2,1,0:T(8,128)S(1)}, f32[1,64,2048]{2,1,0:T(8,128)}, u32[]{:S(2)}) copy-start(f32[1,64,2048]{2,1,0:T(8,128)} %v.2) | copy-start | bytes 1572868
where the time goes:
time: 67.9 us; the launch traced here: 67.8 us
  Pallas kernels  29.4 us (43%)
  starting transfers between devices  23.6 us (35%)
  waiting for transfers between devices  13.4 us (20%)
  between operations  1.09 us (2%)
    pallas_call x17, Pallas kernels, call(): return kernel_call(*args)  29.4 us
    ppermute x4, starting transfers between devices, shifted(): lax.ppermute(x, 'section', [(i, (i + by) % size) for i in range(size)])  14.5 us
    ppermute x4, waiting for transfers between devices, shifted(): lax.ppermute(x, 'section', [(i, (i + by) % size) for i in range(size)])  13.2 us
    ppermute x8, starting transfers between devices, along_x(): lax.ppermute(x, 'dp', [(i, (i // 2 + by) % 4 * 2 + i % 2) for i in range(...  8.41 us
  transfers between devices with their start and end apart: 14, of which 4 were waited for; matrix products, arithmetic and copies ran while one was open for 0% of the time, Pallas kernels for 28%

commit v1 on v0

--- a/solution.py
+++ b/solution.py
@@ -51,8 +51,8 @@
     return lax.dot_general(a, b, (((1,), (1,)), ((), ())), preferred_element_type=F32)
 
 
-def chunks():
-    return [slice(c, c + CHUNK) for c in range(0, FF, CHUNK)]
+def chunks(size=CHUNK):
+    return [slice(c, c + size) for c in range(0, FF, size)]
 
 
 def gelu_both(pre):
@@ -74,9 +74,13 @@
 
 def forward_tick(x, w1, w2, mask):
     acc = ALPHA * x.astype(F32)
-    for c in chunks():
-        h = gelu_both(dot(x, w1[0, :, c]))[0].astype(BF16)
+    columns = chunks(256)
+    pre = dot(x, w1[0, :, columns[0]])
+    for i, c in enumerate(columns):
+        ahead = dot(x, w1[0, :, columns[i + 1]]) if i + 1 < len(columns) else None
+        h = gelu_both(pre)[0].astype(BF16)
         acc = acc + dot_t(h, w2[0, :, c])
+        pre = ahead
     return jnp.where(mask()[:, :1] > 0.0, norm_parts(acc)[0], 0.0).astype(BF16)
 
 
@@ -88,7 +92,8 @@
 
 
 def back_zero_kernel(lens_hbm, w1_hbm, w2_hbm, stash_hbm, cot_hbm,
-                     gin, gp, h, gs, w1, w2, x, slope, cot, lens, sem, w_sem):
+                     gin, gp, h, gs, w1, w2, back_masks, masks,
+                     x, slope, cot, lens, sem, w_sem):
     group, section = lax.axis_index("dp"), lax.axis_index("section")
     get_x = pltpu.make_async_copy(stash_hbm.at[0, 0, 0], x, sem.at[0])
     get_x.start()
@@ -107,21 +112,27 @@
     get_lens.start()
     get_x.wait()
     acc = ALPHA * x[...].astype(F32)
-    for i, c in enumerate(chunks()):
-        get_w1, get_w2 = streams[i]
-        get_w1.wait()
-        if i + 2 < len(streams):
-            streams[i + 2][0].start()
+    pre = None
+    for i in range(len(streams) + 1):
+        if i < len(streams):
+            streams[i][0].wait()
+            if i + 2 < len(streams):
+                streams[i + 2][0].start()
+        if i > 0:
+            streams[i - 1][1].wait()
+            if i + 1 < len(streams):
+                streams[i + 1][1].start()
         if i == 1:
             get_cot.start()
-        value, s = gelu_both(dot(x[...], w1[0, :, c]))
-        value = value.astype(BF16)
-        h[:, c] = value
-        slope[:, c] = s
-        get_w2.wait()
-        if i + 2 < len(streams):
-            streams[i + 2][1].start()
-        acc = acc + dot_t(value, w2[0, :, c])
+        ahead = dot(x[...], w1[0, :, chunks()[i]]) if i < len(streams) else None
+        if i > 0:
+            c = chunks()[i - 1]
+            value, s = gelu_both(pre)
+            value = value.astype(BF16)
+            h[:, c] = value
+            slope[:, c] = s
+            acc = acc + dot_t(value, w2[0, :, c])
+        pre = ahead
     normed, inv = norm_parts(acc)
     get_lens.wait()
     get_cot.wait()
@@ -130,17 +141,22 @@
     total_b = total.astype(BF16)
     gs[...] = total_b
     acc = ALPHA * total
-    for c in chunks():
+    for c in chunks(1024):
         g = (dot(total_b, w2[0, :, c]) * slope[:, c]).astype(BF16)
         gp[:, c] = g
         acc = acc + dot_t(g, w1[0, :, c])
     gin[...] = acc.astype(BF16)
+    last = lax.axis_size("section") - 1
+    for k in (1, 2):
+        back_masks[k - 1] = live(lens[group, section + k]).astype(F32)
+    for k in range(3):
+        masks[k] = live(lens[group, last - section + k]).astype(F32)
 
 
 def prepare(k, w1, w2, stash, masks, h, slope, normed, inv):
     x = stash[0, 0, k]
     acc = ALPHA * x.astype(F32)
-    for c in chunks():
+    for c in chunks(256):
         value, s = gelu_both(dot(x, w1[0, :, c]))
         value = value.astype(BF16)
         h[:, c] = value
@@ -165,7 +181,7 @@
     total_b = total.astype(BF16)
     gs[...] = total_b
     acc = ALPHA * total
-    for c in chunks():
+    for c in chunks(1024):
         g = (dot(total_b, w2[0, :, c]) * slope[:, c]).astype(BF16)
         gp[:, c] = g
         acc = acc + dot_t(g, w1[0, :, c])
@@ -187,16 +203,27 @@
     return jnp.concatenate(parts, axis=0)
 
 
-def terms_kernel(stash, gp0, gp1, gs0, gs1, h0, h1, first, second, x_rows, left):
-    for i, a in enumerate((stash[0, 0, 0], stash[0, 0, 1], gs0[...], gs1[...], stash[0, 0, 2])):
+def terms_zero_kernel(stash, gp, gs, h, first, second, x1_rows, x2_rows, left):
+    for i, a in enumerate((stash[0, 0, 0], gs[...], stash[0, 0, 1], stash[0, 0, 2])):
         left[i] = jnp.transpose(a)
-    a0, a1 = owner_rows(left.at[0]), owner_rows(left.at[1])
+    a = owner_rows(left.at[0])
     for c in chunks():
-        first[:, c] = dot(a0, gp0[:, c]) + dot(a1, gp1[:, c])
-    a0, a1 = owner_rows(left.at[2]), owner_rows(left.at[3])
+        first[:, c] = dot(a, gp[:, c])
+    a = owner_rows(left.at[1])
     for c in chunks():
-        second[:, c] = dot(a0, h0[:, c]) + dot(a1, h1[:, c])
-    x_rows[...] = owner_rows(left.at[4])
+        second[:, c] = dot(a, h[:, c])
+    x1_rows[...] = owner_rows(left.at[2])
+    x2_rows[...] = owner_rows(left.at[3])
+
+
+def terms_one_kernel(x_rows, gp, gs, h, first0, second0, first, second, left):
+    a = x_rows[...]
+    for c in chunks():
+        first[:, c] = first0[:, c] + dot(a, gp[:, c])
+    left[...] = jnp.transpose(gs[...])
+    a = owner_rows(left)
+    for c in chunks():
+        second[:, c] = second0[:, c] + dot(a, h[:, c])
 
 
 def back_two_kernel(passed, loss, normed, inv, h2, second, total_out, keep, send, left):
@@ -214,7 +241,7 @@
 def back_two_first_kernel(w2, total, slope, x_rows, first, gp, keep, send):
     total_b = total[...].astype(BF16)
     a = x_rows[...]
-    for c in chunks():
+    for c in chunks(1024):
         g = (dot(total_b, w2[0, :, c]) * slope[:, c]).astype(BF16)
         gp[:, c] = g
         r = first[:, c] + dot(a, g)
@@ -241,37 +268,25 @@
 def back_leave_kernel(w1, total, gp, gin0, gin1, leave, gin2, sem):
     finish = leaving(leave, (gin0, gin1), gin2, sem)
     acc = ALPHA * total[...]
-    for c in chunks():
+    for c in chunks(2048):
         acc = acc + dot_t(gp[:, c], w1[0, :, c])
     gin2[...] = acc.astype(BF16)
     finish()
 
 
-def forward_zero_kernel(lens_hbm, w1, w2, act, out, back_masks, masks, lens, sem):
-    get_lens = pltpu.make_async_copy(lens_hbm, lens, sem)
-    get_lens.start()
-    group, section = lax.axis_index("dp"), lax.axis_index("section")
-    last = lax.axis_size("section") - 1
-
-    def mask():
-        get_lens.wait()
-        for k in (1, 2):
-            back_masks[k - 1] = live(lens[group, section + k]).astype(F32)
-            masks[k - 1] = live(lens[group, last - section + k]).astype(F32)
-        return live(lens[group, last - section]).astype(F32)
-
-    out[...] = forward_tick(act[0, 0], w1, w2, mask)
+def forward_zero_kernel(w1, w2, act, masks, out):
+    out[...] = forward_tick(act[0, 0], w1, w2, lambda: masks[0])
 
 
 def forward_one_kernel(w1, w2, passed, embed, masks, out):
     x = jnp.where(lax.axis_index("section") == 0, embed[0, 0], passed[...])
-    out[...] = forward_tick(x, w1, w2, lambda: masks[0])
+    out[...] = forward_tick(x, w1, w2, lambda: masks[1])
 
 
 def forward_two_kernel(w1, w2, passed, embed, masks, out0, out1, leave, out2, sem):
     finish = leaving(leave, (out0, out1), out2, sem)
     x = jnp.where(lax.axis_index("section") == 0, embed[0, 1], passed[...])
-    out2[...] = forward_tick(x, w1, w2, lambda: masks[1])
+    out2[...] = forward_tick(x, w1, w2, lambda: masks[2])
     finish()
 
 
@@ -324,22 +339,18 @@
     w1, w2, m_first, v_first, m_second, v_second, lens, act, cot, embed, loss, stash
 ):
     mm = 2 * ROWS * D * FF
-    small, wide, masks2 = (ROWS, D), (ROWS, FF), (2, ROWS, 128)
-    lens_scratch = [pltpu.SMEM(lens.shape, jnp.int32)]
-
-    gin0, gp0, h0, gs0, w1, w2 = call(
+    small, wide = (ROWS, D), (ROWS, FF)
+
+    gin0, gp0, h0, gs0, w1, w2, back_masks, masks = call(
         back_zero_kernel,
-        [(small, BF16), (wide, BF16), (wide, BF16), (small, BF16), (w1.shape, BF16), (w2.shape, BF16)],
+        [(small, BF16), (wide, BF16), (wide, BF16), (small, BF16), (w1.shape, BF16), (w2.shape, BF16),
+         ((2, ROWS, 128), F32), ((3, ROWS, 128), F32)],
         lens, w1, w2, stash, cot, raw=range(5), flops=4 * mm,
         scratch=[pltpu.VMEM(small, BF16), pltpu.VMEM(wide, F32), pltpu.VMEM(small, BF16)]
-        + lens_scratch + [pltpu.SemaphoreType.DMA((3,)), pltpu.SemaphoreType.DMA((2, 4))],
+        + [pltpu.SMEM(lens.shape, jnp.int32), pltpu.SemaphoreType.DMA((3,)),
+           pltpu.SemaphoreType.DMA((2, 4))],
     )
     back1 = shifted(gin0, -1)
-    out0, back_masks, masks = call(
-        forward_zero_kernel, [(small, BF16), (masks2, F32), (masks2, F32)], lens, w1, w2, act,
-        raw=(0,), flops=2 * mm, scratch=lens_scratch + [pltpu.SemaphoreType.DMA],
-    )
-    ahead1 = shifted(out0, 1)
 
     def prepared(kernel):
         return call(
@@ -348,16 +359,23 @@
         )
 
     h1, slope1, normed1, inv1 = prepared(prepare_one_kernel)
+    h2, slope2, normed2, inv2 = prepared(prepare_two_kernel)
+    acc_first, acc_second, x1_rows, x2_rows = call(
+        terms_zero_kernel,
+        [((D, FF), F32), ((D, FF), F32), ((D, ROWS), BF16), ((D, ROWS), BF16)],
+        stash, gp0, gs0, h0, flops=2 * mm, scratch=[pltpu.VMEM((4, D, ROWS), BF16)],
+    )
     gin1, gp1, gs1 = call(
         back_one_kernel, [(small, BF16), (wide, BF16), (small, BF16)],
         w1, w2, back1, loss, slope1, normed1, inv1, flops=2 * mm,
     )
     back2 = shifted(gin1, -1)
-    h2, slope2, normed2, inv2 = prepared(prepare_two_kernel)
-    acc_first, acc_second, x_rows = call(
-        terms_kernel, [((D, FF), F32), ((D, FF), F32), ((D, ROWS), BF16)],
-        stash, gp0, gp1, gs0, gs1, h0, h1, flops=4 * mm,
-        scratch=[pltpu.VMEM((5, D, ROWS), BF16)],
+    (out0,) = call(forward_zero_kernel, [(small, BF16)], w1, w2, act, masks, flops=2 * mm)
+    ahead1 = shifted(out0, 1)
+    acc_first, acc_second = call(
+        terms_one_kernel, [((D, FF), F32), ((D, FF), F32)],
+        x1_rows, gp1, gs1, h1, acc_first, acc_second, flops=2 * mm,
+        scratch=[pltpu.VMEM((D, ROWS), BF16)],
     )
     total2, keep_second, send_second = call(
         back_two_kernel, [(small, F32), ((256, FF), F32), ((256, FF), BF16)],
@@ -367,7 +385,7 @@
     got_second = other_core(send_second)
     gp2, keep_first, send_first = call(
         back_two_first_kernel, [(wide, BF16), ((256, FF), F32), ((256, FF), BF16)],
-        w2, total2, slope2, x_rows, acc_first, flops=2 * mm,
+        w2, total2, slope2, x2_rows, acc_first, flops=2 * mm,
     )
     got_first = other_core(send_first)
     (out1,) = call(

time: 67.9 us -> 67.5 us (level)
  the two profiles are of different devices: /device:TPU:6 before, /device:TPU:4 now
where the time goes in v1:
time: 67.5 us; the launch traced here: 67.3 us
  Pallas kernels  25.9 us (38%)
  starting transfers between devices  23.9 us (35%)
  waiting for transfers between devices  16.2 us (24%)
  between operations  1.11 us (2%)
    pallas_call x18, Pallas kernels, call(): return kernel_call(*args)  25.9 us
    ppermute x4, waiting for transfers between devices, shifted(): lax.ppermute(x, 'section', [(i, (i + by) % size) for i in range(size)])  16.2 us
    ppermute x4, starting transfers between devices, shifted(): lax.ppermute(x, 'section', [(i, (i + by) % size) for i in range(size)])  14.6 us
    ppermute x8, starting transfers between devices, along_x(): lax.ppermute(x, 'dp', [(i, (i // 2 + by) % 4 * 2 + i % 2) for i in range(...  8.63 us
  transfers between devices with their start and end apart: 14, of which 3 were waited for; matrix products, arithmetic and copies ran while one was open for 0% of the time, Pallas kernels for 24%

profile of v1, /device:TPU:4, one launch (start us, length us, event | category | flops | bytes accessed | tf_op | source)
XLA Modules:
  0.0 67.3 jit_solution(13078636267205330593)
XLA Ops:
  0.6 5.9 %shard_map.147 = (bf16[256,512]{1,0:T(8,128)(2,1)S(1)}, bf16[256,2048]{1,0:T(8,128)(2,1)S(1)}, bf16[256,2048]{1,0:T(8,128)(2,1)S(1)}, bf16[256,512]{1,0:T(8,128)...) custom-call(s32[8,34]{1,0:T(8,128)} %lens_hbm.1, ...), custom_call_target="tpu_custom_call" | custom-call | flops 2147483648 | tf_op jit(solution)/shard_map/pallas_call | solution.py:43
  6.5 8.4 %collective-permute-start.2 = (bf16[256,512]{1,0:T(8,128)(2,1)S(1)}, bf16[256,512]{1,0:T(8,128)(2,1)S(1)}, u32[]{:S(2)}, u32[]{:S(2)}) collective-permute-start(bf16[256,512]{1,0:T(8,128)(2,1)S(1)} %get-tuple-element.52.gin0), channel_id=1, source_target_pairs={{0,248},{8,0},{16,8},{24,16},{32,24},{40,32},{48,40},{56,48},{64,5... | collective-permute-start | bytes 786440 | tf_op jit(solution)/shard_map/ppermute | solution.py:327
  14.9 1.9 %shard_map.151 = (bf16[256,2048]{1,0:T(8,128)(2,1)S(1)}, f32[256,2048]{1,0:T(8,128)S(1)}, f32[256,512]{1,0:T(8,128)S(1)}, f32[256,128]{1,0:T(8,128)S(1)}) custom-call(bf16[1,512,2048]{2,1,0:T(8,128)(2,1)S(1)} %get-tuple-element.49.w1.refs_0_, bf16[1,512,2048]{2,1,0:T(8,128)(2,1)S(1)} %get-tuple-element.50.w2.refs_1_, ...), custom_call_target="tpu_custom_call" | custom-call | flops 1073741824 | tf_op jit(solution)/shard_map/pallas_call | solution.py:43
  16.8 3.7 %collective-permute-done.2.passed = bf16[256,512]{1,0:T(8,128)(2,1)S(1)} collective-permute-done((bf16[256,512]{1,0:T(8,128)(2,1)S(1)}, bf16[256,512]{1,0:T(8,128)(2,1)S(1)}, u32[]{:S(2)}, u32[]{:S(2)}) %collective-permute-start.2) | collective-permute-done | bytes 262176 | tf_op jit(solution)/shard_map/ppermute | solution.py:327
  20.5 1.4 %shard_map.152 = (bf16[256,512]{1,0:T(8,128)(2,1)S(1)}, bf16[256,2048]{1,0:T(8,128)(2,1)S(1)}, bf16[256,512]{1,0:T(8,128)(2,1)S(1)}) custom-call(bf16[1,512,2048]{2,1,0:T(8,128)(2,1)S(1)} %get-tuple-element.49.w1.refs_0_, bf16[1,512,2048]{2,1,0:T(8,128)(2,1)S(1)} %get-tuple-element.50.w2.refs_1_, bf16[256,512]{1,0:T(8,128)(2,1)S(1)} %collective-permute-done.2.passed, ...), custom_call_target="tpu_custom_call" | custom-call | flops 1073741824 | tf_op jit(solution)/shard_map/pallas_call | solution.py:43
  21.9 6.1 %collective-permute-start.3 = (bf16[256,512]{1,0:T(8,128)(2,1)S(1)}, bf16[256,512]{1,0:T(8,128)(2,1)S(1)}, u32[]{:S(2)}, u32[]{:S(2)}) collective-permute-start(bf16[256,512]{1,0:T(8,128)(2,1)S(1)} %get-tuple-element.57.gin1), channel_id=1, source_target_pairs={{0,248},{8,0},{16,8},{24,16},{32,24},{40,32},{48,40},{56,48},{64,5... | collective-permute-start | bytes 786440 | tf_op jit(solution)/shard_map/ppermute | solution.py:327
  28.0 1.9 %shard_map.153 = (bf16[256,2048]{1,0:T(8,128)(2,1)S(1)}, f32[256,2048]{1,0:T(8,128)S(1)}, f32[256,512]{1,0:T(8,128)S(1)}, f32[256,128]{1,0:T(8,128)S(1)}) custom-call(bf16[1,512,2048]{2,1,0:T(8,128)(2,1)S(1)} %get-tuple-element.49.w1.refs_0_, bf16[1,512,2048]{2,1,0:T(8,128)(2,1)S(1)} %get-tuple-element.50.w2.refs_1_, ...), custom_call_target="tpu_custom_call" | custom-call | flops 1073741824 | tf_op jit(solution)/shard_map/pallas_call | solution.py:43
  29.9 1.6 %shard_map.154 = (f32[512,2048]{1,0:T(8,128)S(1)}, f32[512,2048]{1,0:T(8,128)S(1)}, bf16[512,256]{1,0:T(8,128)(2,1)S(1)}, bf16[512,256]{1,0:T(8,128)(2,1)S(1)}) custom-call(bf16[1,1,3,256,512]{4,3,2,1,0:T(8,128)(2,1)S(1)} %copy-done, bf16[256,2048]{1,0:T(8,128)(2,1)S(1)} %get-tuple-element.61.gp, bf16[256,512]{1,0:T(8,128)(2,1)S(1)} %get-tuple-element.62.gs, ...), custom_call_target="tpu_custom_call" | custom-call | flops 1073741824 | tf_op jit(solution)/shard_map/pallas_call | solution.py:43
  31.4 1.3 %shard_map.155 = (f32[512,2048]{1,0:T(8,128)S(1)}, f32[512,2048]{1,0:T(8,128)S(1)}) custom-call(bf16[512,256]{1,0:T(8,128)(2,1)S(1)} %get-tuple-element.64.x_rows, bf16[256,2048]{1,0:T(8,128)(2,1)S(1)} %get-tuple-element.65.gp, bf16[256,512]{1,0:T(8,128)(2,1)S(1)} %get-tuple-element.66.gs, bf16[256,2048]{1,0:T(8,128)(2,1)S(1)} %get-tuple-element.67.h, ...), custom_call_target="tpu_custom_call" | custom-call | flops 1073741824 | tf_op jit(solution)/shard_map/pallas_call | solution.py:43
  32.7 1.0 %shard_map.156 = (f32[256,512]{1,0:T(8,128)S(1)}, f32[256,2048]{1,0:T(8,128)S(1)}, bf16[256,2048]{1,0:T(8,128)(2,1)S(1)}) custom-call(bf16[256,512]{1,0:T(8,128)(2,1)S(1)} %collective-permute-done.3.passed, bf16[1,2,256,512]{3,2,1,0:T(8,128)(2,1)S(1)} %copy-done.2, f32[256,512]{1,0:T(8,128)S(1)} %get-tuple-element.58.normed, ...), custom_call_target="tpu_custom_call" | custom-call | flops 536870912 | tf_op jit(solution)/shard_map/pallas_call | solution.py:43
  33.8 0.1 collective-permute-start.9
  33.9 1.3 %shard_map.157 = (bf16[256,2048]{1,0:T(8,128)(2,1)S(1)}, f32[256,2048]{1,0:T(8,128)S(1)}, bf16[256,2048]{1,0:T(8,128)(2,1)S(1)}) custom-call(bf16[1,512,2048]{2,1,0:T(8,128)(2,1)S(1)} %get-tuple-element.50.w2.refs_1_, f32[256,512]{1,0:T(8,128)S(1)} %get-tuple-element.71.total, f32[256,2048]{1,0:T(8,128)S(1)} %get-tuple-element.72.slope, ...), custom_call_target="tpu_custom_call" | custom-call | flops 1073741824 | tf_op jit(solution)/shard_map/pallas_call | solution.py:43
  35.1 0.6 collective-permute-start.4
  35.7 1.6 %shard_map.148.out0 = bf16[256,512]{1,0:T(8,128)(2,1)S(1)} custom-call(bf16[1,512,2048]{2,1,0:T(8,128)(2,1)S(1)} %get-tuple-element.49.w1.refs_0_, bf16[1,512,2048]{2,1,0:T(8,128)(2,1)S(1)} %get-tuple-element.50.w2.refs_1_, bf16[1,1,256,512]{3,2,1,0:T(8,128)(2,1)S(1)} %copy-done.7, f32[3,256,128]{2,1,0:T(8,128)S(1)} %get-tuple-element.51.masks), custom_call_target="tpu_custom_call" | custom-call | flops 1073741824 | tf_op jit(solution)/shard_map/pallas_call | solution.py:43
  37.4 0.2 shard_map.162
  37.6 1.3 %collective-permute-start.10 = (bf16[64,2048]{1,0:T(8,128)(2,1)S(1)}, bf16[64,2048]{1,0:T(8,128)(2,1)S(1)}, u32[]{:S(2)}, u32[]{:S(2)}) collective-permute-start(bf16[64,2048]{1,0:T(8,128)(2,1)S(1)} %get-tuple-element.89), channel_id=1, source_target_pairs={{0,2},{1,3},{2,4},{3,5},{4,6},{5,7},{6,0},{7,1},{8,10},{9,11},{10,... | collective-permute-start | bytes 786440 | tf_op jit(solution)/shard_map/ppermute | solution.py:331
  38.9 0.8 %collective-permute-start.11 = (bf16[64,2048]{1,0:T(8,128)(2,1)S(1)}, bf16[64,2048]{1,0:T(8,128)(2,1)S(1)}, u32[]{:S(2)}, u32[]{:S(2)}) collective-permute-start(bf16[64,2048]{1,0:T(8,128)(2,1)S(1)} %get-tuple-element.90), channel_id=1, source_target_pairs={{0,6},{1,7},{2,0},{3,1},{4,2},{5,3},{6,4},{7,5},{8,14},{9,15},{10,... | collective-permute-start | bytes 786440 | tf_op jit(solution)/shard_map/ppermute | solution.py:331
  39.7 0.2 shard_map.159
  39.9 1.5 %collective-permute-start.5 = (bf16[64,2048]{1,0:T(8,128)(2,1)S(1)}, bf16[64,2048]{1,0:T(8,128)(2,1)S(1)}, u32[]{:S(2)}, u32[]{:S(2)}) collective-permute-start(bf16[64,2048]{1,0:T(8,128)(2,1)S(1)} %get-tuple-element.80), channel_id=1, source_target_pairs={{0,2},{1,3},{2,4},{3,5},{4,6},{5,7},{6,0},{7,1},{8,10},{9,11},{10,... | collective-permute-start | bytes 786440 | tf_op jit(solution)/shard_map/ppermute | solution.py:331
  41.4 0.8 %collective-permute-start.6 = (bf16[64,2048]{1,0:T(8,128)(2,1)S(1)}, bf16[64,2048]{1,0:T(8,128)(2,1)S(1)}, u32[]{:S(2)}, u32[]{:S(2)}) collective-permute-start(bf16[64,2048]{1,0:T(8,128)(2,1)S(1)} %get-tuple-element.81), channel_id=1, source_target_pairs={{0,6},{1,7},{2,0},{3,1},{4,2},{5,3},{6,4},{7,5},{8,14},{9,15},{10,... | collective-permute-start | bytes 786440 | tf_op jit(solution)/shard_map/ppermute | solution.py:331
  42.2 7.5 %collective-permute-done.passed = bf16[256,512]{1,0:T(8,128)(2,1)S(1)} collective-permute-done((bf16[256,512]{1,0:T(8,128)(2,1)S(1)}, bf16[256,512]{1,0:T(8,128)(2,1)S(1)}, u32[]{:S(2)}, u32[]{:S(2)}) %collective-permute-start) | collective-permute-done | bytes 262176 | tf_op jit(solution)/shard_map/ppermute | solution.py:327
  49.7 1.6 %shard_map.149.out1 = bf16[256,512]{1,0:T(8,128)(2,1)S(1)} custom-call(bf16[1,512,2048]{2,1,0:T(8,128)(2,1)S(1)} %get-tuple-element.49.w1.refs_0_, bf16[1,512,2048]{2,1,0:T(8,128)(2,1)S(1)} %get-tuple-element.50.w2.refs_1_, bf16[256,512]{1,0:T(8,128)(2,1)S(1)} %collective-permute-done.passed, bf16[1,2,256,512]{3,2,1,0:T(8,128)(2,1)S(1)} %copy-done.1, ...), custom_call_target="tpu_custom_call" | custom-call | flops 1073741824 | tf_op jit(solution)/shard_map/pallas_call | solution.py:43
  51.5 1.3 %collective-permute-start.12 = (bf16[32,2048]{1,0:T(8,128)(2,1)S(1)}, bf16[32,2048]{1,0:T(8,128)(2,1)S(1)}, u32[]{:S(2)}, u32[]{:S(2)}) collective-permute-start(bf16[32,2048]{1,0:T(8,128)(2,1)S(1)} %get-tuple-element.92), channel_id=1, source_target_pairs={{0,2},{1,3},{2,4},{3,5},{4,6},{5,7},{6,0},{7,1},{8,10},{9,11},{10,... | collective-permute-start | bytes 393224 | tf_op jit(solution)/shard_map/ppermute | solution.py:331
  52.8 0.8 %collective-permute-start.13 = (bf16[32,2048]{1,0:T(8,128)(2,1)S(1)}, bf16[32,2048]{1,0:T(8,128)(2,1)S(1)}, u32[]{:S(2)}, u32[]{:S(2)}) collective-permute-start(bf16[32,2048]{1,0:T(8,128)(2,1)S(1)} %get-tuple-element.93), channel_id=1, source_target_pairs={{0,6},{1,7},{2,0},{3,1},{4,2},{5,3},{6,4},{7,5},{8,14},{9,15},{10,... | collective-permute-start | bytes 393224 | tf_op jit(solution)/shard_map/ppermute | solution.py:331
  53.7 1.3 %collective-permute-start.7 = (bf16[32,2048]{1,0:T(8,128)(2,1)S(1)}, bf16[32,2048]{1,0:T(8,128)(2,1)S(1)}, u32[]{:S(2)}, u32[]{:S(2)}) collective-permute-start(bf16[32,2048]{1,0:T(8,128)(2,1)S(1)} %get-tuple-element.83), channel_id=1, source_target_pairs={{0,2},{1,3},{2,4},{3,5},{4,6},{5,7},{6,0},{7,1},{8,10},{9,11},{10,... | collective-permute-start | bytes 393224 | tf_op jit(solution)/shard_map/ppermute | solution.py:331
  55.0 0.8 %collective-permute-start.8 = (bf16[32,2048]{1,0:T(8,128)(2,1)S(1)}, bf16[32,2048]{1,0:T(8,128)(2,1)S(1)}, u32[]{:S(2)}, u32[]{:S(2)}) collective-permute-start(bf16[32,2048]{1,0:T(8,128)(2,1)S(1)} %get-tuple-element.84), channel_id=1, source_target_pairs={{0,6},{1,7},{2,0},{3,1},{4,2},{5,3},{6,4},{7,5},{8,14},{9,15},{10,... | collective-permute-start | bytes 393224 | tf_op jit(solution)/shard_map/ppermute | solution.py:331
  55.8 1.5 %shard_map.158 = bf16[1,1,3,256,512]{4,3,2,1,0:T(8,128)(2,1)} custom-call(bf16[1,512,2048]{2,1,0:T(8,128)(2,1)S(1)} %get-tuple-element.49.w1.refs_0_, f32[256,512]{1,0:T(8,128)S(1)} %get-tuple-element.71.total, bf16[256,2048]{1,0:T(8,128)(2,1)S(1)} %get-tuple-element.75.gp, bf16[256,512]{1,0:T(8,128)(2,1)S(1)} %get-tuple-element.52.gin0, ...), custom_call_target="tpu_custom_call" | custom-call | flops 536870912 | tf_op jit(solution)/shard_map/pallas_call | solution.py:43
  57.3 5.0 %collective-permute-done.1.passed = bf16[256,512]{1,0:T(8,128)(2,1)S(1)} collective-permute-done((bf16[256,512]{1,0:T(8,128)(2,1)S(1)}, bf16[256,512]{1,0:T(8,128)(2,1)S(1)}, u32[]{:S(2)}, u32[]{:S(2)}) %collective-permute-start.1) | collective-permute-done | bytes 262176 | tf_op jit(solution)/shard_map/ppermute | solution.py:327
  62.4 2.3 %shard_map.150 = bf16[1,1,3,256,512]{4,3,2,1,0:T(8,128)(2,1)} custom-call(bf16[1,512,2048]{2,1,0:T(8,128)(2,1)S(1)} %get-tuple-element.49.w1.refs_0_, bf16[1,512,2048]{2,1,0:T(8,128)(2,1)S(1)} %get-tuple-element.50.w2.refs_1_, bf16[256,512]{1,0:T(8,128)(2,1)S(1)} %collective-permute-done.1.passed, bf16[1,2,256,512]{3,2,1,0:T(8,128)(2,1)S(1)} %copy-done.1, ...), custom_call_target="tpu_custom_call" | custom-call | flops 1073741824 | tf_op jit(solution)/shard_map/pallas_call | solution.py:43
  64.8 1.1 %shard_map.164 = f32[1,64,2048]{2,1,0:T(8,128)} custom-call(f32[64,2048]{1,0:T(8,128)S(1)} %get-tuple-element.91.part, bf16[32,2048]{1,0:T(8,128)(2,1)S(1)} %collective-permute-done.12.got_up, bf16[32,2048]{1,0:T(8,128)(2,1)S(1)} %collective-permute-done.13.got_down, f32[1,64,2048]{2,1,0:T(8,128)S(1)} %copy-done.3, f32[1,64,2048]{2,1,0:T(8,128)S(1)} %copy-done.4), custom_call_target="tpu_custom_call" | custom-call | tf_op jit(solution)/shard_map/pallas_call | solution.py:43
  65.9 0.2 copy-done.6
  66.1 1.1 %shard_map.161 = f32[1,64,2048]{2,1,0:T(8,128)} custom-call(f32[64,2048]{1,0:T(8,128)S(1)} %get-tuple-element.82.part, bf16[32,2048]{1,0:T(8,128)(2,1)S(1)} %collective-permute-done.7.got_up, bf16[32,2048]{1,0:T(8,128)(2,1)S(1)} %collective-permute-done.8.got_down, f32[1,64,2048]{2,1,0:T(8,128)S(1)} %copy-done.5, f32[1,64,2048]{2,1,0:T(8,128)S(1)} %copy-done.6), custom_call_target="tpu_custom_call" | custom-call | tf_op jit(solution)/shard_map/pallas_call | solution.py:43
  (30 shorter events, 0.4 us)
Async XLA Ops:
  0.6 14.3 %copy-start = (bf16[1,1,3,256,512]{4,3,2,1,0:T(8,128)(2,1)S(1)}, bf16[1,1,3,256,512]{4,3,2,1,0:T(8,128)(2,1)}, u32[]{:S(2)}) copy-start(bf16[1,1,3,256,512]{4,3,2,1,0:T(8,128)(2,1)} %stash.1) | copy-start | bytes 2359300
  6.5 14.0 %collective-permute-start.2 = (bf16[256,512]{1,0:T(8,128)(2,1)S(1)}, bf16[256,512]{1,0:T(8,128)(2,1)S(1)}, u32[]{:S(2)}, u32[]{:S(2)}) collective-permute-start(bf16[256,512]{1,0:T(8,128)(2,1)S(1)} %get-tuple-element.52.gin0), channel_id=1, source_target_pairs={{0,248},{8,0},{16,8},{24,16},{32,24},{40,32},{48,40},{56,48},{64,5... | collective-permute-start | bytes 786440 | tf_op jit(solution)/shard_map/ppermute | solution.py:327
  14.9 5.6 %copy-start.2 = (bf16[1,2,256,512]{3,2,1,0:T(8,128)(2,1)S(1)}, bf16[1,2,256,512]{3,2,1,0:T(8,128)(2,1)}, u32[]{:S(2)}) copy-start(bf16[1,2,256,512]{3,2,1,0:T(8,128)(2,1)} %loss.3) | copy-start | bytes 1572868
  21.9 10.8 %collective-permute-start.3 = (bf16[256,512]{1,0:T(8,128)(2,1)S(1)}, bf16[256,512]{1,0:T(8,128)(2,1)S(1)}, u32[]{:S(2)}, u32[]{:S(2)}) collective-permute-start(bf16[256,512]{1,0:T(8,128)(2,1)S(1)} %get-tuple-element.57.gin1), channel_id=1, source_target_pairs={{0,248},{8,0},{16,8},{24,16},{32,24},{40,32},{48,40},{56,48},{64,5... | collective-permute-start | bytes 786440 | tf_op jit(solution)/shard_map/ppermute | solution.py:327
  33.8 3.7 %collective-permute-start.9 = (bf16[256,2048]{1,0:T(8,128)(2,1)S(1)}, bf16[256,2048]{1,0:T(8,128)(2,1)S(1)}, u32[]{:S(2)}, u32[]{:S(2)}) collective-permute-start(bf16[256,2048]{1,0:T(8,128)(2,1)S(1)} %get-tuple-element.86), channel_id=1, source_target_pairs={{0,1},{1,0},{2,3},{3,2},{4,5},{5,4},{6,7},{7,6},{8,9},{9,8},{10,11... | collective-permute-start | bytes 3145736 | tf_op jit(solution)/shard_map/ppermute | solution.py:335
  33.9 1.9 %copy-start.7 = (bf16[1,1,256,512]{3,2,1,0:T(8,128)(2,1)S(1)}, bf16[1,1,256,512]{3,2,1,0:T(8,128)(2,1)}, u32[]{:S(2)}) copy-start(bf16[1,1,256,512]{3,2,1,0:T(8,128)(2,1)} %act.1) | copy-start | bytes 786436
  35.1 4.6 %collective-permute-start.4 = (bf16[256,2048]{1,0:T(8,128)(2,1)S(1)}, bf16[256,2048]{1,0:T(8,128)(2,1)S(1)}, u32[]{:S(2)}, u32[]{:S(2)}) collective-permute-start(bf16[256,2048]{1,0:T(8,128)(2,1)S(1)} %get-tuple-element.77), channel_id=1, source_target_pairs={{0,1},{1,0},{2,3},{3,2},{4,5},{5,4},{6,7},{7,6},{8,9},{9,8},{10,11... | collective-permute-start | bytes 3145736 | tf_op jit(solution)/shard_map/ppermute | solution.py:335
  37.3 12.3 %collective-permute-start = (bf16[256,512]{1,0:T(8,128)(2,1)S(1)}, bf16[256,512]{1,0:T(8,128)(2,1)S(1)}, u32[]{:S(2)}, u32[]{:S(2)}) collective-permute-start(bf16[256,512]{1,0:T(8,128)(2,1)S(1)} %shard_map.148.out0), channel_id=1, source_target_pairs={{0,8},{8,16},{16,24},{24,32},{32,40},{40,48},{48,56},{56,64},{64,7... | collective-permute-start | bytes 786440 | tf_op jit(solution)/shard_map/ppermute | solution.py:327
  37.6 12.1 %copy-start.1 = (bf16[1,2,256,512]{3,2,1,0:T(8,128)(2,1)S(1)}, bf16[1,2,256,512]{3,2,1,0:T(8,128)(2,1)}, u32[]{:S(2)}) copy-start(bf16[1,2,256,512]{3,2,1,0:T(8,128)(2,1)} %embed.3) | copy-start | bytes 1572868
  37.6 13.8 %collective-permute-start.10 = (bf16[64,2048]{1,0:T(8,128)(2,1)S(1)}, bf16[64,2048]{1,0:T(8,128)(2,1)S(1)}, u32[]{:S(2)}, u32[]{:S(2)}) collective-permute-start(bf16[64,2048]{1,0:T(8,128)(2,1)S(1)} %get-tuple-element.89), channel_id=1, source_target_pairs={{0,2},{1,3},{2,4},{3,5},{4,6},{5,7},{6,0},{7,1},{8,10},{9,11},{10,... | collective-permute-start | bytes 786440 | tf_op jit(solution)/shard_map/ppermute | solution.py:331
  38.9 12.5 %collective-permute-start.11 = (bf16[64,2048]{1,0:T(8,128)(2,1)S(1)}, bf16[64,2048]{1,0:T(8,128)(2,1)S(1)}, u32[]{:S(2)}, u32[]{:S(2)}) collective-permute-start(bf16[64,2048]{1,0:T(8,128)(2,1)S(1)} %get-tuple-element.90), channel_id=1, source_target_pairs={{0,6},{1,7},{2,0},{3,1},{4,2},{5,3},{6,4},{7,5},{8,14},{9,15},{10,... | collective-permute-start | bytes 786440 | tf_op jit(solution)/shard_map/ppermute | solution.py:331
  39.9 13.7 %collective-permute-start.5 = (bf16[64,2048]{1,0:T(8,128)(2,1)S(1)}, bf16[64,2048]{1,0:T(8,128)(2,1)S(1)}, u32[]{:S(2)}, u32[]{:S(2)}) collective-permute-start(bf16[64,2048]{1,0:T(8,128)(2,1)S(1)} %get-tuple-element.80), channel_id=1, source_target_pairs={{0,2},{1,3},{2,4},{3,5},{4,6},{5,7},{6,0},{7,1},{8,10},{9,11},{10,... | collective-permute-start | bytes 786440 | tf_op jit(solution)/shard_map/ppermute | solution.py:331
  41.4 12.2 %collective-permute-start.6 = (bf16[64,2048]{1,0:T(8,128)(2,1)S(1)}, bf16[64,2048]{1,0:T(8,128)(2,1)S(1)}, u32[]{:S(2)}, u32[]{:S(2)}) collective-permute-start(bf16[64,2048]{1,0:T(8,128)(2,1)S(1)} %get-tuple-element.81), channel_id=1, source_target_pairs={{0,6},{1,7},{2,0},{3,1},{4,2},{5,3},{6,4},{7,5},{8,14},{9,15},{10,... | collective-permute-start | bytes 786440 | tf_op jit(solution)/shard_map/ppermute | solution.py:331
  51.3 11.1 %collective-permute-start.1 = (bf16[256,512]{1,0:T(8,128)(2,1)S(1)}, bf16[256,512]{1,0:T(8,128)(2,1)S(1)}, u32[]{:S(2)}, u32[]{:S(2)}) collective-permute-start(bf16[256,512]{1,0:T(8,128)(2,1)S(1)} %shard_map.149.out1), channel_id=1, source_target_pairs={{0,8},{8,16},{16,24},{24,32},{32,40},{40,48},{48,56},{56,64},{64,7... | collective-permute-start | bytes 786440 | tf_op jit(solution)/shard_map/ppermute | solution.py:327
  51.5 13.2 %collective-permute-start.12 = (bf16[32,2048]{1,0:T(8,128)(2,1)S(1)}, bf16[32,2048]{1,0:T(8,128)(2,1)S(1)}, u32[]{:S(2)}, u32[]{:S(2)}) collective-permute-start(bf16[32,2048]{1,0:T(8,128)(2,1)S(1)} %get-tuple-element.92), channel_id=1, source_target_pairs={{0,2},{1,3},{2,4},{3,5},{4,6},{5,7},{6,0},{7,1},{8,10},{9,11},{10,... | collective-permute-start | bytes 393224 | tf_op jit(solution)/shard_map/ppermute | solution.py:331
  52.8 12.0 %collective-permute-start.13 = (bf16[32,2048]{1,0:T(8,128)(2,1)S(1)}, bf16[32,2048]{1,0:T(8,128)(2,1)S(1)}, u32[]{:S(2)}, u32[]{:S(2)}) collective-permute-start(bf16[32,2048]{1,0:T(8,128)(2,1)S(1)} %get-tuple-element.93), channel_id=1, source_target_pairs={{0,6},{1,7},{2,0},{3,1},{4,2},{5,3},{6,4},{7,5},{8,14},{9,15},{10,... | collective-permute-start | bytes 393224 | tf_op jit(solution)/shard_map/ppermute | solution.py:331
  53.7 12.1 %collective-permute-start.7 = (bf16[32,2048]{1,0:T(8,128)(2,1)S(1)}, bf16[32,2048]{1,0:T(8,128)(2,1)S(1)}, u32[]{:S(2)}, u32[]{:S(2)}) collective-permute-start(bf16[32,2048]{1,0:T(8,128)(2,1)S(1)} %get-tuple-element.83), channel_id=1, source_target_pairs={{0,2},{1,3},{2,4},{3,5},{4,6},{5,7},{6,0},{7,1},{8,10},{9,11},{10,... | collective-permute-start | bytes 393224 | tf_op jit(solution)/shard_map/ppermute | solution.py:331
  55.0 10.9 %collective-permute-start.8 = (bf16[32,2048]{1,0:T(8,128)(2,1)S(1)}, bf16[32,2048]{1,0:T(8,128)(2,1)S(1)}, u32[]{:S(2)}, u32[]{:S(2)}) collective-permute-start(bf16[32,2048]{1,0:T(8,128)(2,1)S(1)} %get-tuple-element.84), channel_id=1, source_target_pairs={{0,6},{1,7},{2,0},{3,1},{4,2},{5,3},{6,4},{7,5},{8,14},{9,15},{10,... | collective-permute-start | bytes 393224 | tf_op jit(solution)/shard_map/ppermute | solution.py:331
  57.3 7.5 %copy-start.3 = (f32[1,64,2048]{2,1,0:T(8,128)S(1)}, f32[1,64,2048]{2,1,0:T(8,128)}, u32[]{:S(2)}) copy-start(f32[1,64,2048]{2,1,0:T(8,128)} %m.3) | copy-start | bytes 1572868
  57.3 7.5 %copy-start.4 = (f32[1,64,2048]{2,1,0:T(8,128)S(1)}, f32[1,64,2048]{2,1,0:T(8,128)}, u32[]{:S(2)}) copy-start(f32[1,64,2048]{2,1,0:T(8,128)} %v.3) | copy-start | bytes 1572868
  64.7 1.2 %copy-start.5 = (f32[1,64,2048]{2,1,0:T(8,128)S(1)}, f32[1,64,2048]{2,1,0:T(8,128)}, u32[]{:S(2)}) copy-start(f32[1,64,2048]{2,1,0:T(8,128)} %m.2) | copy-start | bytes 1572868
  64.7 1.4 %copy-start.6 = (f32[1,64,2048]{2,1,0:T(8,128)S(1)}, f32[1,64,2048]{2,1,0:T(8,128)}, u32[]{:S(2)}) copy-start(f32[1,64,2048]{2,1,0:T(8,128)} %v.2) | copy-start | bytes 1572868

commit v2 on v1

--- a/solution.py
+++ b/solution.py
@@ -322,9 +322,10 @@
         copy.wait()
 
 
-def shifted(x, by):
+def shifted(x, by, closed=True):
     size = lax.axis_size("section")
-    return lax.ppermute(x, "section", [(i, (i + by) % size) for i in range(size)])
+    pairs = [(i, (i + by) % size) for i in range(size) if closed or 0 <= i + by < size]
+    return lax.ppermute(x, "section", pairs)
 
 
 def along_x(x, by):
@@ -369,7 +370,7 @@
         back_one_kernel, [(small, BF16), (wide, BF16), (small, BF16)],
         w1, w2, back1, loss, slope1, normed1, inv1, flops=2 * mm,
     )
-    back2 = shifted(gin1, -1)
+    back2 = shifted(gin1, -1, closed=False)
     (out0,) = call(forward_zero_kernel, [(small, BF16)], w1, w2, act, masks, flops=2 * mm)
     ahead1 = shifted(out0, 1)
     acc_first, acc_second = call(

time: 67.5 us -> 64.8 us (0.960)
  starting transfers between devices: 23.9 us -> 19.3 us
  waiting for transfers between devices: 16.2 us -> 18.1 us
    ppermute x4, starting transfers between devices: 14.6 us -> 10 us  [shifted(): return lax.ppermute(x, 'section', pairs)]
    ppermute x4, waiting for transfers between devices: 16.2 us -> 18.1 us  [shifted(): return lax.ppermute(x, 'section', pairs)]
  transfers between devices with their start and end apart: 14 -> 14, of which waited for: 3 -> 4; matrix products, arithmetic and copies ran while one was open for 0% -> 0% of each run, Pallas kernels for 24% -> 25%
where the time goes in v2:
time: 64.8 us; the launch traced here: 64.6 us
  Pallas kernels  25.8 us (40%)
  starting transfers between devices  19.3 us (30%)
  waiting for transfers between devices  18.1 us (28%)
  between operations  1.11 us (2%)
    pallas_call x18, Pallas kernels, call(): return kernel_call(*args)  25.8 us
    ppermute x4, waiting for transfers between devices, shifted(): return lax.ppermute(x, 'section', pairs)  18.1 us
    ppermute x4, starting transfers between devices, shifted(): return lax.ppermute(x, 'section', pairs)  10 us
    ppermute x8, starting transfers between devices, along_x(): lax.ppermute(x, 'dp', [(i, (i // 2 + by) % 4 * 2 + i % 2) for i in range(...  8.63 us
  transfers between devices with their start and end apart: 14, of which 4 were waited for; matrix products, arithmetic and copies ran while one was open for 0% of the time, Pallas kernels for 25%

profile of v2, /device:TPU:4, one launch (start us, length us, event | category | flops | bytes accessed | tf_op | source)
XLA Modules:
  0.0 64.6 jit_solution(9233839661687424806)
XLA Ops:
  0.6 5.9 %shard_map.147 = (bf16[256,512]{1,0:T(8,128)(2,1)S(1)}, bf16[256,2048]{1,0:T(8,128)(2,1)S(1)}, bf16[256,2048]{1,0:T(8,128)(2,1)S(1)}, bf16[256,512]{1,0:T(8,128)...) custom-call(s32[8,34]{1,0:T(8,128)} %lens_hbm.1, ...), custom_call_target="tpu_custom_call" | custom-call | flops 2147483648 | tf_op jit(solution)/shard_map/pallas_call | solution.py:43
  6.5 8.4 %collective-permute-start.2 = (bf16[256,512]{1,0:T(8,128)(2,1)S(1)}, bf16[256,512]{1,0:T(8,128)(2,1)S(1)}, u32[]{:S(2)}, u32[]{:S(2)}) collective-permute-start(bf16[256,512]{1,0:T(8,128)(2,1)S(1)} %get-tuple-element.52.gin0), channel_id=1, source_target_pairs={{0,248},{8,0},{16,8},{24,16},{32,24},{40,32},{48,40},{56,48},{64,5... | collective-permute-start | bytes 786440 | tf_op jit(solution)/shard_map/ppermute | solution.py:328
  14.9 1.9 %shard_map.151 = (bf16[256,2048]{1,0:T(8,128)(2,1)S(1)}, f32[256,2048]{1,0:T(8,128)S(1)}, f32[256,512]{1,0:T(8,128)S(1)}, f32[256,128]{1,0:T(8,128)S(1)}) custom-call(bf16[1,512,2048]{2,1,0:T(8,128)(2,1)S(1)} %get-tuple-element.49.w1.refs_0_, bf16[1,512,2048]{2,1,0:T(8,128)(2,1)S(1)} %get-tuple-element.50.w2.refs_1_, ...), custom_call_target="tpu_custom_call" | custom-call | flops 1073741824 | tf_op jit(solution)/shard_map/pallas_call | solution.py:43
  16.8 3.7 %collective-permute-done.2.passed = bf16[256,512]{1,0:T(8,128)(2,1)S(1)} collective-permute-done((bf16[256,512]{1,0:T(8,128)(2,1)S(1)}, bf16[256,512]{1,0:T(8,128)(2,1)S(1)}, u32[]{:S(2)}, u32[]{:S(2)}) %collective-permute-start.2) | collective-permute-done | bytes 262176 | tf_op jit(solution)/shard_map/ppermute | solution.py:328
  20.5 1.4 %shard_map.152 = (bf16[256,512]{1,0:T(8,128)(2,1)S(1)}, bf16[256,2048]{1,0:T(8,128)(2,1)S(1)}, bf16[256,512]{1,0:T(8,128)(2,1)S(1)}) custom-call(bf16[1,512,2048]{2,1,0:T(8,128)(2,1)S(1)} %get-tuple-element.49.w1.refs_0_, bf16[1,512,2048]{2,1,0:T(8,128)(2,1)S(1)} %get-tuple-element.50.w2.refs_1_, bf16[256,512]{1,0:T(8,128)(2,1)S(1)} %collective-permute-done.2.passed, ...), custom_call_target="tpu_custom_call" | custom-call | flops 1073741824 | tf_op jit(solution)/shard_map/pallas_call | solution.py:43
  21.9 1.5 %collective-permute-start.3 = (bf16[256,512]{1,0:T(8,128)(2,1)S(1)}, bf16[256,512]{1,0:T(8,128)(2,1)S(1)}, u32[]{:S(2)}, u32[]{:S(2)}) collective-permute-start(bf16[256,512]{1,0:T(8,128)(2,1)S(1)} %get-tuple-element.57.gin1), channel_id=1, source_target_pairs={{8,0},{16,8},{24,16},{32,24},{40,32},{48,40},{56,48},{64,56},{72,6... | collective-permute-start | bytes 786440 | tf_op jit(solution)/shard_map/ppermute | solution.py:328
  23.4 1.9 %shard_map.153 = (bf16[256,2048]{1,0:T(8,128)(2,1)S(1)}, f32[256,2048]{1,0:T(8,128)S(1)}, f32[256,512]{1,0:T(8,128)S(1)}, f32[256,128]{1,0:T(8,128)S(1)}) custom-call(bf16[1,512,2048]{2,1,0:T(8,128)(2,1)S(1)} %get-tuple-element.49.w1.refs_0_, bf16[1,512,2048]{2,1,0:T(8,128)(2,1)S(1)} %get-tuple-element.50.w2.refs_1_, ...), custom_call_target="tpu_custom_call" | custom-call | flops 1073741824 | tf_op jit(solution)/shard_map/pallas_call | solution.py:43
  25.3 1.6 %shard_map.154 = (f32[512,2048]{1,0:T(8,128)S(1)}, f32[512,2048]{1,0:T(8,128)S(1)}, bf16[512,256]{1,0:T(8,128)(2,1)S(1)}, bf16[512,256]{1,0:T(8,128)(2,1)S(1)}) custom-call(bf16[1,1,3,256,512]{4,3,2,1,0:T(8,128)(2,1)S(1)} %copy-done, bf16[256,2048]{1,0:T(8,128)(2,1)S(1)} %get-tuple-element.61.gp, bf16[256,512]{1,0:T(8,128)(2,1)S(1)} %get-tuple-element.62.gs, ...), custom_call_target="tpu_custom_call" | custom-call | flops 1073741824 | tf_op jit(solution)/shard_map/pallas_call | solution.py:43
  26.9 1.3 %shard_map.155 = (f32[512,2048]{1,0:T(8,128)S(1)}, f32[512,2048]{1,0:T(8,128)S(1)}) custom-call(bf16[512,256]{1,0:T(8,128)(2,1)S(1)} %get-tuple-element.64.x_rows, bf16[256,2048]{1,0:T(8,128)(2,1)S(1)} %get-tuple-element.65.gp, bf16[256,512]{1,0:T(8,128)(2,1)S(1)} %get-tuple-element.66.gs, bf16[256,2048]{1,0:T(8,128)(2,1)S(1)} %get-tuple-element.67.h, ...), custom_call_target="tpu_custom_call" | custom-call | flops 1073741824 | tf_op jit(solution)/shard_map/pallas_call | solution.py:43
  28.1 2.9 %collective-permute-done.3.passed = bf16[256,512]{1,0:T(8,128)(2,1)S(1)} collective-permute-done((bf16[256,512]{1,0:T(8,128)(2,1)S(1)}, bf16[256,512]{1,0:T(8,128)(2,1)S(1)}, u32[]{:S(2)}, u32[]{:S(2)}) %collective-permute-start.3) | collective-permute-done | bytes 262176 | tf_op jit(solution)/shard_map/ppermute | solution.py:328
  31.0 1.0 %shard_map.156 = (f32[256,512]{1,0:T(8,128)S(1)}, f32[256,2048]{1,0:T(8,128)S(1)}, bf16[256,2048]{1,0:T(8,128)(2,1)S(1)}) custom-call(bf16[256,512]{1,0:T(8,128)(2,1)S(1)} %collective-permute-done.3.passed, bf16[1,2,256,512]{3,2,1,0:T(8,128)(2,1)S(1)} %copy-done.2, f32[256,512]{1,0:T(8,128)S(1)} %get-tuple-element.58.normed, ...), custom_call_target="tpu_custom_call" | custom-call | flops 536870912 | tf_op jit(solution)/shard_map/pallas_call | solution.py:43
  32.2 1.3 %shard_map.157 = (bf16[256,2048]{1,0:T(8,128)(2,1)S(1)}, f32[256,2048]{1,0:T(8,128)S(1)}, bf16[256,2048]{1,0:T(8,128)(2,1)S(1)}) custom-call(bf16[1,512,2048]{2,1,0:T(8,128)(2,1)S(1)} %get-tuple-element.50.w2.refs_1_, f32[256,512]{1,0:T(8,128)S(1)} %get-tuple-element.71.total, f32[256,2048]{1,0:T(8,128)S(1)} %get-tuple-element.72.slope, ...), custom_call_target="tpu_custom_call" | custom-call | flops 1073741824 | tf_op jit(solution)/shard_map/pallas_call | solution.py:43
  33.4 0.6 collective-permute-start.4
  34.0 1.6 %shard_map.148.out0 = bf16[256,512]{1,0:T(8,128)(2,1)S(1)} custom-call(bf16[1,512,2048]{2,1,0:T(8,128)(2,1)S(1)} %get-tuple-element.49.w1.refs_0_, bf16[1,512,2048]{2,1,0:T(8,128)(2,1)S(1)} %get-tuple-element.50.w2.refs_1_, bf16[1,1,256,512]{3,2,1,0:T(8,128)(2,1)S(1)} %copy-done.7, f32[3,256,128]{2,1,0:T(8,128)S(1)} %get-tuple-element.51.masks), custom_call_target="tpu_custom_call" | custom-call | flops 1073741824 | tf_op jit(solution)/shard_map/pallas_call | solution.py:43
  35.7 0.2 shard_map.162
  35.9 1.3 %collective-permute-start.10 = (bf16[64,2048]{1,0:T(8,128)(2,1)S(1)}, bf16[64,2048]{1,0:T(8,128)(2,1)S(1)}, u32[]{:S(2)}, u32[]{:S(2)}) collective-permute-start(bf16[64,2048]{1,0:T(8,128)(2,1)S(1)} %get-tuple-element.89), channel_id=1, source_target_pairs={{0,2},{1,3},{2,4},{3,5},{4,6},{5,7},{6,0},{7,1},{8,10},{9,11},{10,... | collective-permute-start | bytes 786440 | tf_op jit(solution)/shard_map/ppermute | solution.py:332
  37.2 0.8 %collective-permute-start.11 = (bf16[64,2048]{1,0:T(8,128)(2,1)S(1)}, bf16[64,2048]{1,0:T(8,128)(2,1)S(1)}, u32[]{:S(2)}, u32[]{:S(2)}) collective-permute-start(bf16[64,2048]{1,0:T(8,128)(2,1)S(1)} %get-tuple-element.90), channel_id=1, source_target_pairs={{0,6},{1,7},{2,0},{3,1},{4,2},{5,3},{6,4},{7,5},{8,14},{9,15},{10,... | collective-permute-start | bytes 786440 | tf_op jit(solution)/shard_map/ppermute | solution.py:332
  38.0 0.2 shard_map.159
  38.2 1.5 %collective-permute-start.5 = (bf16[64,2048]{1,0:T(8,128)(2,1)S(1)}, bf16[64,2048]{1,0:T(8,128)(2,1)S(1)}, u32[]{:S(2)}, u32[]{:S(2)}) collective-permute-start(bf16[64,2048]{1,0:T(8,128)(2,1)S(1)} %get-tuple-element.80), channel_id=1, source_target_pairs={{0,2},{1,3},{2,4},{3,5},{4,6},{5,7},{6,0},{7,1},{8,10},{9,11},{10,... | collective-permute-start | bytes 786440 | tf_op jit(solution)/shard_map/ppermute | solution.py:332
  39.7 0.8 %collective-permute-start.6 = (bf16[64,2048]{1,0:T(8,128)(2,1)S(1)}, bf16[64,2048]{1,0:T(8,128)(2,1)S(1)}, u32[]{:S(2)}, u32[]{:S(2)}) collective-permute-start(bf16[64,2048]{1,0:T(8,128)(2,1)S(1)} %get-tuple-element.81), channel_id=1, source_target_pairs={{0,6},{1,7},{2,0},{3,1},{4,2},{5,3},{6,4},{7,5},{8,14},{9,15},{10,... | collective-permute-start | bytes 786440 | tf_op jit(solution)/shard_map/ppermute | solution.py:332
  40.5 6.7 %collective-permute-done.passed = bf16[256,512]{1,0:T(8,128)(2,1)S(1)} collective-permute-done((bf16[256,512]{1,0:T(8,128)(2,1)S(1)}, bf16[256,512]{1,0:T(8,128)(2,1)S(1)}, u32[]{:S(2)}, u32[]{:S(2)}) %collective-permute-start) | collective-permute-done | bytes 262176 | tf_op jit(solution)/shard_map/ppermute | solution.py:328
  47.3 1.6 %shard_map.149.out1 = bf16[256,512]{1,0:T(8,128)(2,1)S(1)} custom-call(bf16[1,512,2048]{2,1,0:T(8,128)(2,1)S(1)} %get-tuple-element.49.w1.refs_0_, bf16[1,512,2048]{2,1,0:T(8,128)(2,1)S(1)} %get-tuple-element.50.w2.refs_1_, bf16[256,512]{1,0:T(8,128)(2,1)S(1)} %collective-permute-done.passed, bf16[1,2,256,512]{3,2,1,0:T(8,128)(2,1)S(1)} %copy-done.1, ...), custom_call_target="tpu_custom_call" | custom-call | flops 1073741824 | tf_op jit(solution)/shard_map/pallas_call | solution.py:43
  49.1 1.3 %collective-permute-start.12 = (bf16[32,2048]{1,0:T(8,128)(2,1)S(1)}, bf16[32,2048]{1,0:T(8,128)(2,1)S(1)}, u32[]{:S(2)}, u32[]{:S(2)}) collective-permute-start(bf16[32,2048]{1,0:T(8,128)(2,1)S(1)} %get-tuple-element.92), channel_id=1, source_target_pairs={{0,2},{1,3},{2,4},{3,5},{4,6},{5,7},{6,0},{7,1},{8,10},{9,11},{10,... | collective-permute-start | bytes 393224 | tf_op jit(solution)/shard_map/ppermute | solution.py:332
  50.3 0.8 %collective-permute-start.13 = (bf16[32,2048]{1,0:T(8,128)(2,1)S(1)}, bf16[32,2048]{1,0:T(8,128)(2,1)S(1)}, u32[]{:S(2)}, u32[]{:S(2)}) collective-permute-start(bf16[32,2048]{1,0:T(8,128)(2,1)S(1)} %get-tuple-element.93), channel_id=1, source_target_pairs={{0,6},{1,7},{2,0},{3,1},{4,2},{5,3},{6,4},{7,5},{8,14},{9,15},{10,... | collective-permute-start | bytes 393224 | tf_op jit(solution)/shard_map/ppermute | solution.py:332
  51.3 1.3 %collective-permute-start.7 = (bf16[32,2048]{1,0:T(8,128)(2,1)S(1)}, bf16[32,2048]{1,0:T(8,128)(2,1)S(1)}, u32[]{:S(2)}, u32[]{:S(2)}) collective-permute-start(bf16[32,2048]{1,0:T(8,128)(2,1)S(1)} %get-tuple-element.83), channel_id=1, source_target_pairs={{0,2},{1,3},{2,4},{3,5},{4,6},{5,7},{6,0},{7,1},{8,10},{9,11},{10,... | collective-permute-start | bytes 393224 | tf_op jit(solution)/shard_map/ppermute | solution.py:332
  52.6 0.8 %collective-permute-start.8 = (bf16[32,2048]{1,0:T(8,128)(2,1)S(1)}, bf16[32,2048]{1,0:T(8,128)(2,1)S(1)}, u32[]{:S(2)}, u32[]{:S(2)}) collective-permute-start(bf16[32,2048]{1,0:T(8,128)(2,1)S(1)} %get-tuple-element.84), channel_id=1, source_target_pairs={{0,6},{1,7},{2,0},{3,1},{4,2},{5,3},{6,4},{7,5},{8,14},{9,15},{10,... | collective-permute-start | bytes 393224 | tf_op jit(solution)/shard_map/ppermute | solution.py:332
  53.4 1.5 %shard_map.158 = bf16[1,1,3,256,512]{4,3,2,1,0:T(8,128)(2,1)} custom-call(bf16[1,512,2048]{2,1,0:T(8,128)(2,1)S(1)} %get-tuple-element.49.w1.refs_0_, f32[256,512]{1,0:T(8,128)S(1)} %get-tuple-element.71.total, bf16[256,2048]{1,0:T(8,128)(2,1)S(1)} %get-tuple-element.75.gp, bf16[256,512]{1,0:T(8,128)(2,1)S(1)} %get-tuple-element.52.gin0, ...), custom_call_target="tpu_custom_call" | custom-call | flops 536870912 | tf_op jit(solution)/shard_map/pallas_call | solution.py:43
  54.9 4.8 %collective-permute-done.1.passed = bf16[256,512]{1,0:T(8,128)(2,1)S(1)} collective-permute-done((bf16[256,512]{1,0:T(8,128)(2,1)S(1)}, bf16[256,512]{1,0:T(8,128)(2,1)S(1)}, u32[]{:S(2)}, u32[]{:S(2)}) %collective-permute-start.1) | collective-permute-done | bytes 262176 | tf_op jit(solution)/shard_map/ppermute | solution.py:328
  59.7 2.3 %shard_map.150 = bf16[1,1,3,256,512]{4,3,2,1,0:T(8,128)(2,1)} custom-call(bf16[1,512,2048]{2,1,0:T(8,128)(2,1)S(1)} %get-tuple-element.49.w1.refs_0_, bf16[1,512,2048]{2,1,0:T(8,128)(2,1)S(1)} %get-tuple-element.50.w2.refs_1_, bf16[256,512]{1,0:T(8,128)(2,1)S(1)} %collective-permute-done.1.passed, bf16[1,2,256,512]{3,2,1,0:T(8,128)(2,1)S(1)} %copy-done.1, ...), custom_call_target="tpu_custom_call" | custom-call | flops 1073741824 | tf_op jit(solution)/shard_map/pallas_call | solution.py:43
  62.1 1.1 %shard_map.164 = f32[1,64,2048]{2,1,0:T(8,128)} custom-call(f32[64,2048]{1,0:T(8,128)S(1)} %get-tuple-element.91.part, bf16[32,2048]{1,0:T(8,128)(2,1)S(1)} %collective-permute-done.12.got_up, bf16[32,2048]{1,0:T(8,128)(2,1)S(1)} %collective-permute-done.13.got_down, f32[1,64,2048]{2,1,0:T(8,128)S(1)} %copy-done.3, f32[1,64,2048]{2,1,0:T(8,128)S(1)} %copy-done.4), custom_call_target="tpu_custom_call" | custom-call | tf_op jit(solution)/shard_map/pallas_call | solution.py:43
  63.2 0.2 copy-done.6
  63.4 1.1 %shard_map.161 = f32[1,64,2048]{2,1,0:T(8,128)} custom-call(f32[64,2048]{1,0:T(8,128)S(1)} %get-tuple-element.82.part, bf16[32,2048]{1,0:T(8,128)(2,1)S(1)} %collective-permute-done.7.got_up, bf16[32,2048]{1,0:T(8,128)(2,1)S(1)} %collective-permute-done.8.got_down, f32[1,64,2048]{2,1,0:T(8,128)S(1)} %copy-done.5, f32[1,64,2048]{2,1,0:T(8,128)S(1)} %copy-done.6), custom_call_target="tpu_custom_call" | custom-call | tf_op jit(solution)/shard_map/pallas_call | solution.py:43
  (30 shorter events, 0.5 us)
Async XLA Ops:
  0.6 14.3 %copy-start = (bf16[1,1,3,256,512]{4,3,2,1,0:T(8,128)(2,1)S(1)}, bf16[1,1,3,256,512]{4,3,2,1,0:T(8,128)(2,1)}, u32[]{:S(2)}) copy-start(bf16[1,1,3,256,512]{4,3,2,1,0:T(8,128)(2,1)} %stash.1) | copy-start | bytes 2359300
  6.5 14.0 %collective-permute-start.2 = (bf16[256,512]{1,0:T(8,128)(2,1)S(1)}, bf16[256,512]{1,0:T(8,128)(2,1)S(1)}, u32[]{:S(2)}, u32[]{:S(2)}) collective-permute-start(bf16[256,512]{1,0:T(8,128)(2,1)S(1)} %get-tuple-element.52.gin0), channel_id=1, source_target_pairs={{0,248},{8,0},{16,8},{24,16},{32,24},{40,32},{48,40},{56,48},{64,5... | collective-permute-start | bytes 786440 | tf_op jit(solution)/shard_map/ppermute | solution.py:328
  14.9 5.6 %copy-start.2 = (bf16[1,2,256,512]{3,2,1,0:T(8,128)(2,1)S(1)}, bf16[1,2,256,512]{3,2,1,0:T(8,128)(2,1)}, u32[]{:S(2)}) copy-start(bf16[1,2,256,512]{3,2,1,0:T(8,128)(2,1)} %loss.3) | copy-start | bytes 1572868
  21.9 9.1 %collective-permute-start.3 = (bf16[256,512]{1,0:T(8,128)(2,1)S(1)}, bf16[256,512]{1,0:T(8,128)(2,1)S(1)}, u32[]{:S(2)}, u32[]{:S(2)}) collective-permute-start(bf16[256,512]{1,0:T(8,128)(2,1)S(1)} %get-tuple-element.57.gin1), channel_id=1, source_target_pairs={{8,0},{16,8},{24,16},{32,24},{40,32},{48,40},{56,48},{64,56},{72,6... | collective-permute-start | bytes 786440 | tf_op jit(solution)/shard_map/ppermute | solution.py:328
  32.0 3.7 %collective-permute-start.9 = (bf16[256,2048]{1,0:T(8,128)(2,1)S(1)}, bf16[256,2048]{1,0:T(8,128)(2,1)S(1)}, u32[]{:S(2)}, u32[]{:S(2)}) collective-permute-start(bf16[256,2048]{1,0:T(8,128)(2,1)S(1)} %get-tuple-element.86), channel_id=1, source_target_pairs={{0,1},{1,0},{2,3},{3,2},{4,5},{5,4},{6,7},{7,6},{8,9},{9,8},{10,11... | collective-permute-start | bytes 3145736 | tf_op jit(solution)/shard_map/ppermute | solution.py:336
  32.1 1.9 %copy-start.7 = (bf16[1,1,256,512]{3,2,1,0:T(8,128)(2,1)S(1)}, bf16[1,1,256,512]{3,2,1,0:T(8,128)(2,1)}, u32[]{:S(2)}) copy-start(bf16[1,1,256,512]{3,2,1,0:T(8,128)(2,1)} %act.1) | copy-start | bytes 786436
  33.4 4.6 %collective-permute-start.4 = (bf16[256,2048]{1,0:T(8,128)(2,1)S(1)}, bf16[256,2048]{1,0:T(8,128)(2,1)S(1)}, u32[]{:S(2)}, u32[]{:S(2)}) collective-permute-start(bf16[256,2048]{1,0:T(8,128)(2,1)S(1)} %get-tuple-element.77), channel_id=1, source_target_pairs={{0,1},{1,0},{2,3},{3,2},{4,5},{5,4},{6,7},{7,6},{8,9},{9,8},{10,11... | collective-permute-start | bytes 3145736 | tf_op jit(solution)/shard_map/ppermute | solution.py:336
  35.6 11.6 %collective-permute-start = (bf16[256,512]{1,0:T(8,128)(2,1)S(1)}, bf16[256,512]{1,0:T(8,128)(2,1)S(1)}, u32[]{:S(2)}, u32[]{:S(2)}) collective-permute-start(bf16[256,512]{1,0:T(8,128)(2,1)S(1)} %shard_map.148.out0), channel_id=1, source_target_pairs={{0,8},{8,16},{16,24},{24,32},{32,40},{40,48},{48,56},{56,64},{64,7... | collective-permute-start | bytes 786440 | tf_op jit(solution)/shard_map/ppermute | solution.py:328
  35.9 11.4 %copy-start.1 = (bf16[1,2,256,512]{3,2,1,0:T(8,128)(2,1)S(1)}, bf16[1,2,256,512]{3,2,1,0:T(8,128)(2,1)}, u32[]{:S(2)}) copy-start(bf16[1,2,256,512]{3,2,1,0:T(8,128)(2,1)} %embed.3) | copy-start | bytes 1572868
  35.9 13.1 %collective-permute-start.10 = (bf16[64,2048]{1,0:T(8,128)(2,1)S(1)}, bf16[64,2048]{1,0:T(8,128)(2,1)S(1)}, u32[]{:S(2)}, u32[]{:S(2)}) collective-permute-start(bf16[64,2048]{1,0:T(8,128)(2,1)S(1)} %get-tuple-element.89), channel_id=1, source_target_pairs={{0,2},{1,3},{2,4},{3,5},{4,6},{5,7},{6,0},{7,1},{8,10},{9,11},{10,... | collective-permute-start | bytes 786440 | tf_op jit(solution)/shard_map/ppermute | solution.py:332
  37.2 11.8 %collective-permute-start.11 = (bf16[64,2048]{1,0:T(8,128)(2,1)S(1)}, bf16[64,2048]{1,0:T(8,128)(2,1)S(1)}, u32[]{:S(2)}, u32[]{:S(2)}) collective-permute-start(bf16[64,2048]{1,0:T(8,128)(2,1)S(1)} %get-tuple-element.90), channel_id=1, source_target_pairs={{0,6},{1,7},{2,0},{3,1},{4,2},{5,3},{6,4},{7,5},{8,14},{9,15},{10,... | collective-permute-start | bytes 786440 | tf_op jit(solution)/shard_map/ppermute | solution.py:332
  38.2 13.0 %collective-permute-start.5 = (bf16[64,2048]{1,0:T(8,128)(2,1)S(1)}, bf16[64,2048]{1,0:T(8,128)(2,1)S(1)}, u32[]{:S(2)}, u32[]{:S(2)}) collective-permute-start(bf16[64,2048]{1,0:T(8,128)(2,1)S(1)} %get-tuple-element.80), channel_id=1, source_target_pairs={{0,2},{1,3},{2,4},{3,5},{4,6},{5,7},{6,0},{7,1},{8,10},{9,11},{10,... | collective-permute-start | bytes 786440 | tf_op jit(solution)/shard_map/ppermute | solution.py:332
  39.7 11.5 %collective-permute-start.6 = (bf16[64,2048]{1,0:T(8,128)(2,1)S(1)}, bf16[64,2048]{1,0:T(8,128)(2,1)S(1)}, u32[]{:S(2)}, u32[]{:S(2)}) collective-permute-start(bf16[64,2048]{1,0:T(8,128)(2,1)S(1)} %get-tuple-element.81), channel_id=1, source_target_pairs={{0,6},{1,7},{2,0},{3,1},{4,2},{5,3},{6,4},{7,5},{8,14},{9,15},{10,... | collective-permute-start | bytes 786440 | tf_op jit(solution)/shard_map/ppermute | solution.py:332
  48.9 10.8 %collective-permute-start.1 = (bf16[256,512]{1,0:T(8,128)(2,1)S(1)}, bf16[256,512]{1,0:T(8,128)(2,1)S(1)}, u32[]{:S(2)}, u32[]{:S(2)}) collective-permute-start(bf16[256,512]{1,0:T(8,128)(2,1)S(1)} %shard_map.149.out1), channel_id=1, source_target_pairs={{0,8},{8,16},{16,24},{24,32},{32,40},{40,48},{48,56},{56,64},{64,7... | collective-permute-start | bytes 786440 | tf_op jit(solution)/shard_map/ppermute | solution.py:328
  49.1 12.9 %collective-permute-start.12 = (bf16[32,2048]{1,0:T(8,128)(2,1)S(1)}, bf16[32,2048]{1,0:T(8,128)(2,1)S(1)}, u32[]{:S(2)}, u32[]{:S(2)}) collective-permute-start(bf16[32,2048]{1,0:T(8,128)(2,1)S(1)} %get-tuple-element.92), channel_id=1, source_target_pairs={{0,2},{1,3},{2,4},{3,5},{4,6},{5,7},{6,0},{7,1},{8,10},{9,11},{10,... | collective-permute-start | bytes 393224 | tf_op jit(solution)/shard_map/ppermute | solution.py:332
  50.3 11.7 %collective-permute-start.13 = (bf16[32,2048]{1,0:T(8,128)(2,1)S(1)}, bf16[32,2048]{1,0:T(8,128)(2,1)S(1)}, u32[]{:S(2)}, u32[]{:S(2)}) collective-permute-start(bf16[32,2048]{1,0:T(8,128)(2,1)S(1)} %get-tuple-element.93), channel_id=1, source_target_pairs={{0,6},{1,7},{2,0},{3,1},{4,2},{5,3},{6,4},{7,5},{8,14},{9,15},{10,... | collective-permute-start | bytes 393224 | tf_op jit(solution)/shard_map/ppermute | solution.py:332
  51.3 11.9 %collective-permute-start.7 = (bf16[32,2048]{1,0:T(8,128)(2,1)S(1)}, bf16[32,2048]{1,0:T(8,128)(2,1)S(1)}, u32[]{:S(2)}, u32[]{:S(2)}) collective-permute-start(bf16[32,2048]{1,0:T(8,128)(2,1)S(1)} %get-tuple-element.83), channel_id=1, source_target_pairs={{0,2},{1,3},{2,4},{3,5},{4,6},{5,7},{6,0},{7,1},{8,10},{9,11},{10,... | collective-permute-start | bytes 393224 | tf_op jit(solution)/shard_map/ppermute | solution.py:332
  52.6 10.5 %collective-permute-start.8 = (bf16[32,2048]{1,0:T(8,128)(2,1)S(1)}, bf16[32,2048]{1,0:T(8,128)(2,1)S(1)}, u32[]{:S(2)}, u32[]{:S(2)}) collective-permute-start(bf16[32,2048]{1,0:T(8,128)(2,1)S(1)} %get-tuple-element.84), channel_id=1, source_target_pairs={{0,6},{1,7},{2,0},{3,1},{4,2},{5,3},{6,4},{7,5},{8,14},{9,15},{10,... | collective-permute-start | bytes 393224 | tf_op jit(solution)/shard_map/ppermute | solution.py:332
  54.9 7.2 %copy-start.3 = (f32[1,64,2048]{2,1,0:T(8,128)S(1)}, f32[1,64,2048]{2,1,0:T(8,128)}, u32[]{:S(2)}) copy-start(f32[1,64,2048]{2,1,0:T(8,128)} %m.3) | copy-start | bytes 1572868
  54.9 7.2 %copy-start.4 = (f32[1,64,2048]{2,1,0:T(8,128)S(1)}, f32[1,64,2048]{2,1,0:T(8,128)}, u32[]{:S(2)}) copy-start(f32[1,64,2048]{2,1,0:T(8,128)} %v.3) | copy-start | bytes 1572868
  62.0 1.2 %copy-start.5 = (f32[1,64,2048]{2,1,0:T(8,128)S(1)}, f32[1,64,2048]{2,1,0:T(8,128)}, u32[]{:S(2)}) copy-start(f32[1,64,2048]{2,1,0:T(8,128)} %m.2) | copy-start | bytes 1572868
  62.0 1.4 %copy-start.6 = (f32[1,64,2048]{2,1,0:T(8,128)S(1)}, f32[1,64,2048]{2,1,0:T(8,128)}, u32[]{:S(2)}) copy-start(f32[1,64,2048]{2,1,0:T(8,128)} %v.2) | copy-start | bytes 1572868
